TPU v7x, 256 devices: a whole 4x4x8 slice. The times are simulated.
256 devices in a mesh: req: 64 (over x, z, core), tp: 4 (over y).
Axes of the slice: x: 4, y: 4, z: 8, core: 2. Of those that a mesh axis runs over, the one named last changes fastest.
Arguments:
- queries: bfloat16 [512, 2560], P('req', 'tp'), may hold values from -68 to 68, as said below
- new_kv: bfloat16 [512, 4, 256], P('req', 'tp'), may hold values from -6 to 6
- residual: bfloat16 [512, 2560], P('req', 'tp'), may hold values from -6 to 6
- kv_cache: bfloat16 [512, 512, 4, 256], P('req', None, 'tp'), may hold values from -6 to 6
- cache_len: int32 [512], P('req'), may hold values from 1 to 511, as said below
- request_perm: int32 [512], replicated, may hold values from 0 to 511, each once
- expert_ids: int32 [512, 6], P('req'), may hold values from 0 to 63, all different within a row; in each aligned block of 8 rows (0 to 7, 8 to 15, ...) at most 2 rows name the same one
- route_wt: float32 [512, 6], P('req'), may hold values from 0.05 to 1
- attn_out_w: bfloat16 [2560, 2560], P('tp'), may hold values from -0.125 to 0.125
- post_gain: float32 [2560], replicated, may hold values from 0.25 to 1.75
- expert_gate_up: bfloat16 [64, 2, 2560, 1536], P('req', None, None, 'tp'), may hold values from -0.125 to 0.125
- expert_down: bfloat16 [64, 1536, 2560], P('req', 'tp'), may hold values from -0.15625 to 0.15625
- final_gain: float32 [2560], replicated, may hold values from 0.25 to 1.75
- vocab_w: bfloat16 [103424, 2560], P(('req', 'tp')), may hold values from -0.125 to 0.125
Outputs:
- hidden_out: bfloat16 [512, 2560], P('req', 'tp')
- state_norm: float32 [512], P('req')
- top_logit: float32 [512], P('req')
Inputs may be any that keep to these rules, and one draw needn't show every extreme that they name: queries lie within this range. Slot s holds cache_len[s] filled rows; some slot holds exactly 511. `request_perm`: a permutation of the slots. `expert_ids`: each row names 6 different experts; among the rows of one device (aligned blocks of 8 rows) no expert is named more than 2 times, and in some block one expert is named exactly 2 times.
All inputs are finite; a program needn't handle non-finite values.
Results may differ from a plain program's by a relative error of at most 0.007.
Values may be sent and summed in bfloat16 or wider, within the bound.
No kernel may reach another device: no remote copies, remote signals or barrier semaphores. Data moves between devices by JAX's collectives and lax.ppermute only.
A program may use at most 64 MiB of HBM per device.

v0:
```python
import jax
import jax.numpy as jnp
from jax import lax
from jax.sharding import PartitionSpec as P

epsilon = 1e-05


def attend(queries, fresh_kv, kv_block, lengths, head_dim):
    slot_count, context, kv_heads, _ = kv_block.shape
    groups = queries.shape[1] // head_dim // kv_heads
    query_heads = queries.reshape(slot_count, kv_heads, groups, head_dim)
    key_part = kv_block[..., :head_dim]
    value_part = kv_block[..., head_dim:]
    score_scale = head_dim ** (-0.5)
    scores = (
        jnp.einsum("skgd,sckd->skgc", query_heads, key_part, preferred_element_type=jnp.float32)
        * score_scale
    )
    live_mask = (jnp.arange(context, dtype=jnp.int32)[None, :] < lengths[:, None])[:, None, None, :]
    scores = jnp.where(live_mask, scores, -1e30)
    own_score = (
        jnp.einsum(
            "skgd,skd->skg",
            query_heads,
            fresh_kv[..., :head_dim],
            preferred_element_type=jnp.float32,
        )
        * score_scale
    )
    highest = jnp.maximum(jnp.max(scores, axis=-1), own_score)
    weights = jnp.where(live_mask, jnp.exp(scores - highest[..., None]), 0.0)
    own_weight = jnp.exp(own_score - highest)
    total_weight = jnp.sum(weights, axis=-1) + own_weight
    own_round = lax.optimization_barrier(own_weight.astype(jnp.bfloat16)).astype(jnp.float32)
    mixed_sum = jnp.einsum(
        "skgc,sckd->skgd",
        weights.astype(jnp.bfloat16),
        value_part,
        preferred_element_type=jnp.float32,
    )
    mixed_sum = mixed_sum + own_round[..., None] * fresh_kv[:, :, None, head_dim:].astype(
        jnp.float32
    )
    return (mixed_sum / total_weight[..., None]).reshape(slot_count, -1).astype(jnp.bfloat16)


def expert_rows(inputs, gate_up, down_proj):
    gate_val = jnp.dot(inputs, gate_up[0], preferred_element_type=jnp.float32)
    upward = jnp.dot(inputs, gate_up[1], preferred_element_type=jnp.float32)
    active = (jax.nn.silu(gate_val) * upward).astype(jnp.bfloat16)
    return jnp.dot(active, down_proj, preferred_element_type=jnp.float32)


def send_back(results):
    return lax.all_to_all(
        results.astype(jnp.bfloat16), "req", split_axis=0, concat_axis=0, tiled=True
    ).astype(results.dtype)


def on_device(
    queries,
    new_kv,
    residual,
    kv_cache,
    cache_len,
    request_perm,
    expert_ids,
    route_wt,
    attn_out_w,
    post_gain,
    expert_gate_up,
    expert_down,
    final_gain,
    vocab_w,
):
    group_count = lax.axis_size("req")
    group_index = lax.axis_index("req")
    member = lax.axis_index("tp")
    local_rows = queries.shape[0]
    top_count = expert_ids.shape[1]
    col_width = residual.shape[1]
    model_width = attn_out_w.shape[1]
    head_dim = new_kv.shape[2] // 2
    capacity = max(2, (local_rows * top_count + group_count - 1) // group_count)
    dealt_q, dealt_kv, dealt_res = (
        lax.all_gather(queries, "req", axis=0, tiled=True),
        lax.all_gather(new_kv, "req", axis=0, tiled=True),
        lax.all_gather(residual, "req", axis=0, tiled=True),
    )
    total_rows = dealt_q.shape[0]
    slot_ids = group_index * local_rows + jnp.arange(local_rows, dtype=jnp.int32)
    pick_rows = (request_perm[None, :] == slot_ids[:, None]).astype(jnp.bfloat16)
    mine_q = jnp.dot(pick_rows, dealt_q, preferred_element_type=jnp.float32).astype(jnp.bfloat16)
    mine_kv = jnp.dot(
        pick_rows, dealt_kv.reshape(total_rows, -1), preferred_element_type=jnp.float32
    )
    mine_kv = mine_kv.astype(jnp.bfloat16).reshape(new_kv.shape)
    mine_res = jnp.dot(pick_rows, dealt_res, preferred_element_type=jnp.float32)
    attended = attend(mine_q, mine_kv, kv_cache, cache_len, head_dim)
    partial_value = jnp.dot(attended, attn_out_w, preferred_element_type=jnp.float32)
    col_start = member * col_width
    own_part = lax.dynamic_slice_in_dim(partial_value, col_start, col_width, 1) + mine_res
    summand = lax.dynamic_update_slice_in_dim(partial_value, own_part, col_start, 1)
    mixed_full = lax.psum(summand, "tp")
    scale_rows = lax.rsqrt(jnp.mean(mixed_full * mixed_full, axis=1, keepdims=True) + epsilon)
    normed = (mixed_full * scale_rows * post_gain).astype(jnp.bfloat16)
    mixed_cols = lax.dynamic_slice_in_dim(mixed_full, col_start, col_width, 1)
    expert_axis = jnp.arange(group_count, dtype=jnp.int32)
    hit_table = (
        (expert_ids[..., None] == expert_axis)
        .astype(jnp.int32)
        .reshape(local_rows * top_count, group_count)
    )
    earlier = jnp.cumsum(hit_table, axis=0) - hit_table
    slot_rank = jnp.sum(earlier * hit_table, axis=1)
    target = expert_ids.reshape(-1) * capacity + slot_rank
    slot_axis = jnp.arange(group_count * capacity, dtype=jnp.int32)
    matches = (slot_axis[:, None] == target[None, :]).astype(jnp.float32)
    matches = matches.reshape(group_count * capacity, local_rows, top_count)
    route_share = route_wt / jnp.sum(route_wt, axis=1, keepdims=True)
    blending = jnp.sum(matches * route_share[None], axis=2).T
    gate_up = expert_gate_up[0]
    down_proj = expert_down[0]
    every_row = lax.all_gather(normed, "req", axis=0, tiled=True)
    every_id = lax.all_gather(expert_ids, "req", axis=0, tiled=True)
    all_hits = (every_id[..., None] == expert_axis).astype(jnp.int32)
    all_hits = all_hits.reshape(group_count, local_rows * top_count, group_count)
    all_prior = jnp.cumsum(all_hits, axis=1) - all_hits
    all_rank = jnp.sum(all_prior * all_hits, axis=2)
    own_routes = every_id.reshape(group_count, local_rows * top_count) == group_index
    cap_axis = jnp.arange(capacity, dtype=jnp.int32)
    chosen = (own_routes[..., None] & (all_rank[..., None] == cap_axis)).astype(jnp.float32)
    chosen = jnp.sum(chosen.reshape(group_count, local_rows, top_count, capacity), axis=2).astype(
        jnp.bfloat16
    )
    inbound = jnp.einsum(
        "btc,btd->bcd",
        chosen,
        every_row.reshape(group_count, local_rows, model_width),
        preferred_element_type=jnp.float32,
    )
    inbound = inbound.astype(jnp.bfloat16)
    produced = expert_rows(inbound.reshape(group_count * capacity, model_width), gate_up, down_proj)
    returned = send_back(produced.reshape(group_count, capacity, model_width))
    moe_part = jnp.dot(
        blending,
        returned.reshape(group_count * capacity, model_width),
        precision=lax.Precision.HIGHEST,
        preferred_element_type=jnp.float32,
    )
    moe_cols = lax.psum_scatter(
        moe_part.astype(jnp.bfloat16), "tp", scatter_dimension=1, tiled=True
    ).astype(jnp.float32)
    state_cols = (mixed_cols + moe_cols).astype(jnp.bfloat16)
    state_row = lax.all_gather(state_cols, "tp", axis=1, tiled=True)
    every_state = lax.all_gather(state_row, "req", axis=0, tiled=True)
    wanted = lax.dynamic_slice_in_dim(request_perm, group_index * local_rows, local_rows)
    back_pick = wanted[:, None] == jnp.arange(total_rows, dtype=jnp.int32)[None, :]
    own_rows = jnp.dot(
        back_pick.astype(jnp.bfloat16), every_state, preferred_element_type=jnp.float32
    )
    hidden_out = lax.dynamic_slice_in_dim(own_rows, col_start, col_width, 1).astype(jnp.bfloat16)
    state_norm = jnp.sqrt(jnp.mean(own_rows * own_rows, axis=1) + epsilon)
    every_flat = every_state.astype(jnp.float32)
    ready_rows = (
        every_flat
        * lax.rsqrt(jnp.mean(every_flat * every_flat, axis=1, keepdims=True) + epsilon)
        * final_gain
    ).astype(jnp.bfloat16)
    logits = lax.dot_general(
        ready_rows, vocab_w, (((1,), (1,)), ((), ())), preferred_element_type=jnp.float32
    )
    local_top = jnp.max(logits, axis=1)
    global_top = lax.pmax(local_top, ("req", "tp"))
    top_logit = jnp.sum(jnp.where(back_pick, global_top[None, :], 0.0), axis=1)
    return (hidden_out, state_norm, top_logit)


def solution(mesh):
    placed = (
        P("req", "tp"),
        P("req", "tp", None),
        P("req", "tp"),
        P("req", None, "tp", None),
        P("req"),
        P(),
        P("req", None),
        P("req", None),
        P("tp", None),
        P(),
        P("req", None, None, "tp"),
        P("req", "tp", None),
        P(),
        P(("req", "tp"), None),
    )
    return jax.shard_map(
        on_device,
        mesh=mesh,
        in_specs=placed,
        out_specs=(P("req", "tp"), P("req"), P("req")),
        check_vma=False,
    )
```

profile of v0, /device:TPU:1, one launch (start us, length us, event | category | flops | bytes accessed | tf_op | source)
XLA Modules:
  0.0 543.5 jit_solution(1999221724259459225)
XLA Ops:
  7.3 55.1 %all_gather.21 = bf16[512,640]{1,0:T(8,128)(2,1)S(1)} all-gather(bf16[8,640]{1,0:T(8,128)(2,1)} %param.14), channel_id=1, replica_groups=mesh['req'=64,'tp'=4] {'req'}, dimensions={0}, use_global_device_ids=true | all-gather | bytes 665600 | tf_op jit(solution)/shard_map/all_gather | solution.py:87
  62.4 43.1 %all_gather.22 = bf16[512,1,256]{2,0,1:T(8,128)(2,1)S(1)} all-gather(bf16[8,1,256]{2,0,1:T(8,128)(2,1)} %param.15), channel_id=1, replica_groups=mesh['req'=64,'tp'=4] {'req'}, dimensions={0}, use_global_device_ids=true | all-gather | bytes 266240 | tf_op jit(solution)/shard_map/all_gather | solution.py:88
  108.1 1.7 fusion.69
  110.0 52.5 %all_gather.23 = bf16[512,640]{1,0:T(8,128)(2,1)} all-gather(bf16[8,640]{1,0:T(8,128)(2,1)S(1)} %copy-done.7), channel_id=1, replica_groups=mesh['req'=64,'tp'=4] {'req'}, dimensions={0}, use_global_device_ids=true | all-gather | bytes 665600 | tf_op jit(solution)/shard_map/all_gather | solution.py:89
  166.7 40.7 %all-reduce.2.cloned.1.call-done = f32[8,2560]{1,0:T(8,128)} async-done(((f32[8,2560]{1,0:T(8,128)}), f32[8,2560]{1,0:T(8,128)}) %all-reduce.2.cloned.1.call-update) | async-done | bytes 81936 | tf_op jit(solution)/shard_map/psum | solution.py:105
  208.5 1.6 multiply_convert_fusion
  210.1 47.8 %all_gather.24 = s32[512,6]{1,0:T(8,128)S(1)} all-gather(s32[8,6]{1,0:T(8,128)S(1)} %copy-done.4), channel_id=1, replica_groups=mesh['req'=64,'tp'=4] {'req'}, dimensions={0}, use_global_device_ids=true | all-gather | bytes 12480 | tf_op jit(solution)/shard_map/all_gather | solution.py:126
  261.1 1.7 fusion.68
  262.9 28.5 %all-gather.3.cloned.1.call-done = bf16[512,2560]{1,0:T(8,128)(2,1)} async-done(((bf16[8,2560]{1,0:T(8,128)(2,1)}), bf16[512,2560]{1,0:T(8,128)(2,1)}) %all-gather.3.cloned.1.call-update) | async-done | bytes 2621456 | tf_op jit(solution)/shard_map/all_gather | solution.py:125
  291.4 3.4 convolution_convert_fusion
  294.8 2.7 reshape.188
  297.6 2.3 fusion.13
  299.9 2.1 fusion.26
  302.0 2.1 convolution_convert_fusion.1
  305.6 6.7 %all-to-all-start = ((bf16[64,2,2560]{2,1,0:T(2,128)(2,1)}), bf16[64,2,2560]{2,1,0:T(2,128)(2,1)}, u32[]{:S(2)}, u32[]{:S(2)}) async-start(bf16[64,2,2560]{2,1,0:T(2,128)(2,1)} %copy.46), calls=%async_computation | async-start | bytes 1310720 | tf_op jit(solution)/shard_map/all_to_all | solution.py:56
  313.3 19.0 %all-to-all-done = bf16[64,2,2560]{2,1,0:T(2,128)(2,1)} async-done(((bf16[64,2,2560]{2,1,0:T(2,128)(2,1)}), bf16[64,2,2560]{2,1,0:T(2,128)(2,1)}, u32[]{:S(2)}, u32[]{:S(2)}) %all-to-all-start) | async-done | bytes 655392 | tf_op jit(solution)/shard_map/all_to_all | solution.py:56
  332.4 2.7 reshape.189
  337.7 20.3 %reduce-scatter.4.cloned.1.call-done = bf16[640,8]{1,0:T(8,128)(2,1)} async-done(((bf16[2560,8]{1,0:T(8,128)(2,1)}), bf16[640,8]{1,0:T(8,128)(2,1)}) %reduce-scatter.4.cloned.1.call-update) | async-done | bytes 10256
  359.7 9.9 %all_gather.26 = bf16[8,2560]{1,0:T(8,128)(2,1)} all-gather(bf16[8,640]{1,0:T(8,128)(2,1)S(1)} %add_convert_fusion), channel_id=1, replica_groups=mesh['req'=64,'tp'=4] {'tp'}, dimensions={1}, use_global_device_ids=true | all-gather | bytes 51200 | tf_op jit(solution)/shard_map/all_gather | solution.py:156
  369.8 82.1 %all-gather.5.cloned.1.call-done = bf16[512,2560]{1,0:T(8,128)(2,1)} async-done(((bf16[8,2560]{1,0:T(8,128)(2,1)}), bf16[512,2560]{1,0:T(8,128)(2,1)}) %all-gather.5.cloned.1.call-update) | async-done | bytes 2621456 | tf_op jit(solution)/shard_map/all_gather | solution.py:157
  451.9 2.5 fusion
  454.4 3.0 fusion.20
  457.4 75.4 %pmax.7 = f32[512]{0:T(512)S(1)} all-reduce(f32[512]{0:T(512)S(1)} %fusion.20), channel_id=1, replica_groups=mesh['req'=64,'tp'=4] {'req','tp'}, use_global_device_ids=true, to_apply=%region_15.16 | all-reduce | flops 512 | bytes 4096 | tf_op jit(solution)/shard_map/pmax | solution.py:175
  533.5 2.3 multiply_reduce_fusion
  (73 shorter events, 20.3 us)
Async XLA Ops:
  7.2 156.9 %copy-start = (bf16[640,2560]{1,0:T(8,128)(2,1)S(1)}, bf16[640,2560]{1,0:T(8,128)(2,1)}, u32[]{:S(2)}) copy-start(bf16[640,2560]{1,0:T(8,128)(2,1)} %param.22) | copy-start | bytes 9830404
  7.2 102.8 %copy-start.7 = (bf16[8,640]{1,0:T(8,128)(2,1)S(1)}, bf16[8,640]{1,0:T(8,128)(2,1)}, u32[]{:S(2)}) copy-start(bf16[8,640]{1,0:T(8,128)(2,1)} %param.16) | copy-start | bytes 30724
  7.2 200.2 %all-reduce.2.cloned.1.call-start = ((), (), s32[]{:S(2)}) async-start(), calls=%async_computation.2 | async-start | bytes 163840 | tf_op jit(solution)/shard_map/psum | solution.py:105
  162.5 2.1 copy-start.8
  164.1 44.4 %copy-start.6 = (f32[2560]{0:T(1024)S(1)}, f32[2560]{0:T(1024)}, u32[]{:S(2)}) copy-start(f32[2560]{0:T(1024)} %param.23) | copy-start | bytes 30724
  164.1 46.0 %copy-start.4 = (s32[8,6]{1,0:T(8,128)S(1)}, s32[8,6]{1,0:T(8,128)}, u32[]{:S(2)}) copy-start(s32[8,6]{1,0:T(8,128)} %param.20) | copy-start | bytes 580
  166.0 0.6 copy-start.3
  166.6 124.8 %all-gather.3.cloned.1.call-start = ((), (), s32[]{:S(2)}) async-start(), calls=%async_computation.3 | async-start | bytes 2662400 | tf_op jit(solution)/shard_map/all_gather | solution.py:125
  297.5 2.3 copy-start.2
  302.0 10.9 %copy-start.5 = (f32[8,6]{1,0:T(8,128)S(1)}, f32[8,6]{1,0:T(8,128)}, u32[]{:S(2)}) copy-start(f32[8,6]{1,0:T(8,128)} %param.21) | copy-start | bytes 580
  305.6 26.7 %all-to-all-start = ((bf16[64,2,2560]{2,1,0:T(2,128)(2,1)}), bf16[64,2,2560]{2,1,0:T(2,128)(2,1)}, u32[]{:S(2)}, u32[]{:S(2)}) async-start(bf16[64,2,2560]{2,1,0:T(2,128)(2,1)} %copy.46), calls=%async_computation | async-start | bytes 1310720 | tf_op jit(solution)/shard_map/all_to_all | solution.py:56
  312.3 45.7 %reduce-scatter.4.cloned.1.call-start = ((), (), s32[]{:S(2)}) async-start(), calls=%async_computation.5 | async-start | bytes 819200
  336.5 117.8 %copy-start.9 = (f32[2560]{0:T(1024)S(1)}, f32[2560]{0:T(1024)}, u32[]{:S(2)}) copy-start(f32[2560]{0:T(1024)} %param.26) | copy-start | bytes 30724
  337.6 114.2 %all-gather.5.cloned.1.call-start = ((), (), s32[]{:S(2)}) async-start(), calls=%async_computation.4 | async-start | bytes 2662400 | tf_op jit(solution)/shard_map/all_gather | solution.py:157
  451.9 2.5 copy-start.1
Sparse Core Ops, SparseCore 0:
  166.8 40.6 all-reduce.1
  210.6 80.8 all-gather.2
  337.8 20.1 reduce-scatter.3
  369.8 82.0 all-gather.4
where the time goes:
time: 545 us; the launch traced here: 544 us
  blocking collectives  284 us (52%)
  waiting for transfers between devices  191 us (35%)
  matrix products  23.6 us (4%)
  between operations  14 us (3%)
  local copies, waits for them, and re-layouts  13.5 us (2%)
  other arithmetic  11 us (2%)
  starting transfers between devices  6.83 us (1%)
    all_gather x1, waiting for transfers between devices, on_device(): every_state = lax.all_gather(state_row, 'req', axis=0, tiled=True)  82.1 us
    pmax x1, blocking collectives, on_device(): global_top = lax.pmax(local_top, ('req', 'tp'))  75.4 us
    all_gather x1, blocking collectives, on_device(): lax.all_gather(queries, 'req', axis=0, tiled=True)  55.1 us
    all_gather x1, blocking collectives, on_device(): lax.all_gather(residual, 'req', axis=0, tiled=True)  52.5 us
    all_gather x1, blocking collectives, on_device(): every_id = lax.all_gather(expert_ids, 'req', axis=0, tiled=True)  47.8 us
    all_gather x1, blocking collectives, on_device(): lax.all_gather(new_kv, 'req', axis=0, tiled=True)  43.1 us
    psum x1, waiting for transfers between devices, on_device(): mixed_full = lax.psum(summand, 'tp')  40.7 us
    all_gather x1, waiting for transfers between devices, on_device(): every_row = lax.all_gather(normed, 'req', axis=0, tiled=True)  28.5 us
  transfers between devices with their start and end apart: 5, of which 5 were waited for; matrix products, arithmetic and copies ran while one was open for 1% of the time, Pallas kernels for 0%

commit v1 on v0

v1 whole, which is shorter than its diff:
```python
import jax
import jax.numpy as jnp
from jax import lax
from jax.sharding import Mesh, PartitionSpec as P

epsilon = 1e-05
X, Z, C, Y = 4, 8, 2, 4
REQ = ("x", "z", "c")
ALL = ("x", "z", "c", "y")
BF = jnp.bfloat16
F32 = jnp.float32


def attend(queries, fresh_kv, kv_block, lengths, head_dim):
    slot_count, context, kv_heads, _ = kv_block.shape
    groups = queries.shape[1] // head_dim // kv_heads
    query_heads = queries.reshape(slot_count, kv_heads, groups, head_dim)
    key_part = kv_block[..., :head_dim]
    value_part = kv_block[..., head_dim:]
    score_scale = head_dim ** (-0.5)
    scores = (
        jnp.einsum("skgd,sckd->skgc", query_heads, key_part, preferred_element_type=F32)
        * score_scale
    )
    live_mask = (jnp.arange(context, dtype=jnp.int32)[None, :] < lengths[:, None])[:, None, None, :]
    scores = jnp.where(live_mask, scores, -1e30)
    own_score = (
        jnp.einsum(
            "skgd,skd->skg", query_heads, fresh_kv[..., :head_dim], preferred_element_type=F32
        )
        * score_scale
    )
    highest = jnp.maximum(jnp.max(scores, axis=-1), own_score)
    weights = jnp.where(live_mask, jnp.exp(scores - highest[..., None]), 0.0)
    own_weight = jnp.exp(own_score - highest)
    total_weight = jnp.sum(weights, axis=-1) + own_weight
    own_round = lax.reduce_precision(own_weight, 8, 7)
    mixed_sum = jnp.einsum(
        "skgc,sckd->skgd", weights.astype(BF), value_part, preferred_element_type=F32
    )
    mixed_sum = mixed_sum + own_round[..., None] * fresh_kv[:, :, None, head_dim:].astype(F32)
    return (mixed_sum / total_weight[..., None]).reshape(slot_count, -1).astype(BF)


def share(values, axes, count):
    stacked = jnp.broadcast_to(values[None], (count,) + values.shape)
    return lax.all_to_all(stacked, axes, 0, 0, tiled=True)


def on_device(
    queries,
    new_kv,
    residual,
    kv_cache,
    cache_len,
    request_perm,
    expert_ids,
    route_wt,
    attn_out_w,
    post_gain,
    expert_gate_up,
    expert_down,
    final_gain,
    vocab_w,
):
    ix, iz, ic, iy = (lax.axis_index(a) for a in ALL)
    rows = queries.shape[0]
    groups = X * Z * C
    total = groups * rows
    group_index = (ix * Z + iz) * C + ic
    col = residual.shape[1]
    width = attn_out_w.shape[1]
    kv_width = new_kv.shape[2]
    head_dim = kv_width // 2
    top_count = expert_ids.shape[1]
    cap = 2
    int_range = lambda n: jnp.arange(n, dtype=jnp.int32)

    packed = jnp.concatenate([queries, new_kv.reshape(rows, kv_width), residual], axis=1)
    plane = share(packed, ("x", "c"), X * C).reshape(X * C * rows, -1)
    plane_slots = lax.dynamic_index_in_dim(
        request_perm.reshape(X, Z, C * rows), iz, 1, keepdims=False
    ).reshape(-1)
    wanted_slots = (((ix * Z + int_range(Z)) * C + ic) * rows)[:, None] + int_range(rows)[None, :]
    select = (wanted_slots.reshape(-1)[:, None] == plane_slots[None, :]).astype(BF)
    outgoing = jnp.dot(select, plane, preferred_element_type=F32).astype(BF)
    arrived = lax.all_to_all(outgoing.reshape(Z, rows, -1), "z", 0, 0, tiled=True)
    mine = jnp.sum(arrived.astype(F32), axis=0).astype(BF)
    mine_q = mine[:, :col]
    mine_kv = mine[:, col : col + kv_width].reshape(rows, 1, kv_width)
    mine_res = mine[:, col + kv_width :]

    attended = attend(mine_q, mine_kv, kv_cache, cache_len, head_dim)
    partial_value = jnp.dot(attended, attn_out_w, preferred_element_type=F32).astype(BF)
    parts = share(jnp.concatenate([partial_value, mine_res], axis=1), "y", Y)
    full_res = jnp.concatenate([parts[t, :, width:] for t in range(Y)], axis=1).astype(F32)
    mixed_full = full_res + jnp.sum(parts[:, :, :width].astype(F32), axis=0)
    mixed_cols = lax.dynamic_slice_in_dim(mixed_full, iy * col, col, 1)
    scale_rows = lax.rsqrt(jnp.mean(mixed_full * mixed_full, axis=1, keepdims=True) + epsilon)
    normed = (mixed_full * scale_rows * post_gain).astype(BF)

    hits = expert_ids[:, :, None] == int_range(groups)[None, None, :]
    row_hits = jnp.sum(hits.astype(jnp.int32), axis=1)
    rank = jnp.cumsum(row_hits, axis=0) - row_hits
    place = (row_hits[:, :, None] > 0) & (rank[:, :, None] == int_range(cap)[None, None, :])
    place = place.reshape(rows, groups * cap)
    route_share = route_wt / jnp.sum(route_wt, axis=1, keepdims=True)
    row_share = jnp.sum(jnp.where(hits, route_share[:, :, None], 0.0), axis=1)
    blend = jnp.where(
        place,
        jnp.broadcast_to(row_share[:, :, None], (rows, groups, cap)).reshape(rows, -1),
        0.0,
    )
    sent = jnp.dot(place.T.astype(BF), normed, preferred_element_type=F32).astype(BF)
    inbound = lax.all_to_all(sent.reshape(groups, cap, width), REQ, 0, 0, tiled=True)
    inbound = inbound.reshape(groups * cap, width)
    gate_val = jnp.dot(inbound, expert_gate_up[0, 0], preferred_element_type=F32)
    upward = jnp.dot(inbound, expert_gate_up[0, 1], preferred_element_type=F32)
    active = (jax.nn.silu(gate_val) * upward).astype(BF)
    produced = jnp.dot(active, expert_down[0], preferred_element_type=F32).astype(BF)

    produced = produced.reshape(groups, cap, Y, col).transpose(0, 2, 1, 3)
    returned = lax.all_to_all(
        produced.reshape(groups * Y, cap, col), ALL, 0, 0, tiled=True
    ).reshape(groups * Y * cap, col)
    blend = jnp.broadcast_to(
        blend.reshape(rows, groups, 1, cap), (rows, groups, Y, cap)
    ).reshape(rows, -1)
    blend_high = lax.reduce_precision(blend, 8, 7)
    blend_two = jnp.concatenate([blend_high, blend - blend_high], axis=0).astype(BF)
    moe_two = jnp.dot(blend_two, returned, preferred_element_type=F32)
    state_cols = (mixed_cols + moe_two[:rows] + moe_two[rows:]).astype(BF)

    by_zy = share(state_cols, ("z", "y"), Z * Y)
    by_x = share(by_zy, ("x",), X)
    other = lax.ppermute(by_x, "c", [(0, 1), (1, 0)])
    first = jnp.where(ic == 0, by_x, other)
    second = jnp.where(ic == 0, other, by_x)
    every = jnp.stack([first, second]).reshape(C, X, Z, Y, rows, col)
    chunks = [every[:, :, :, t].reshape(total, col) for t in range(Y)]
    slot_of = (
        ((int_range(X)[None, :, None] * Z + int_range(Z)[None, None, :]) * C)
        + int_range(C)[:, None, None]
    )[..., None] * rows + int_range(rows)
    slot_of = slot_of.reshape(-1)
    square = sum(jnp.sum(jnp.square(c.astype(F32)), axis=1) for c in chunks)
    mean_eps = square / width + epsilon
    row_scale = lax.rsqrt(mean_eps)[:, None]
    logits = 0.0
    for t, c in enumerate(chunks):
        ready = (c.astype(F32) * row_scale * final_gain[t * col : (t + 1) * col]).astype(BF)
        logits = logits + lax.dot_general(
            ready,
            vocab_w[:, t * col : (t + 1) * col],
            (((1,), (1,)), ((), ())),
            preferred_element_type=F32,
        )
    local_top = jnp.max(logits, axis=1)
    pick = request_perm[:, None] == slot_of[None, :]
    top_by_request = jnp.sum(jnp.where(pick, local_top[None, :], 0.0), axis=1)
    tops = jnp.broadcast_to(top_by_request.reshape(groups, 1, rows), (groups, Y, rows))
    tops = lax.all_to_all(tops.reshape(groups * Y, rows), ALL, 0, 0, tiled=True)
    top_logit = jnp.max(tops, axis=0)

    wanted = lax.dynamic_slice_in_dim(request_perm, group_index * rows, rows)
    back = wanted[:, None] == slot_of[None, :]
    own_chunk = lax.dynamic_index_in_dim(every, iy, 3, keepdims=False).reshape(total, col)
    hidden_out = jnp.dot(back.astype(BF), own_chunk, preferred_element_type=F32).astype(BF)
    state_norm = jnp.sqrt(jnp.sum(jnp.where(back, mean_eps[None, :], 0.0), axis=1))
    return (hidden_out, state_norm, top_logit)


def solution(mesh):
    fine = Mesh(mesh.devices.reshape(X, Z, C, Y), ALL)
    placed = (
        P(REQ, "y"),
        P(REQ, "y", None),
        P(REQ, "y"),
        P(REQ, None, "y", None),
        P(REQ),
        P(),
        P(REQ, None),
        P(REQ, None),
        P("y", None),
        P(),
        P(REQ, None, None, "y"),
        P(REQ, "y", None),
        P(),
        P(ALL, None),
    )
    return jax.shard_map(
        on_device,
        mesh=fine,
        in_specs=placed,
        out_specs=(P(REQ, "y"), P(REQ), P(REQ)),
        check_vma=False,
    )
```

time: 545 us -> 204 us (0.37)
  blocking collectives: 284 us -> 63.2 us
  waiting for transfers between devices: 191 us -> 51.8 us
  starting transfers between devices: 6.83 us -> 35.9 us
  between operations: 14 us -> 0.93 us
  local copies, waits for them, and re-layouts: 13.5 us -> 19.9 us
    all_gather x5 -> x0, blocking collectives: 208 us -> none  [the longest x1 55.1 us: on_device(): lax.all_gather(queries, 'req', axis=0, tiled=True)]
    all_gather x2 -> x0, waiting for transfers between devices: 111 us -> none  [the longest x1 82.1 us: on_device(): every_state = lax.all_gather(state_row, 'req', axis=0, tiled=True)]
    pmax x1 -> x0, blocking collectives: 75.4 us -> none  [on_device(): global_top = lax.pmax(local_top, ('req', 'tp'))]
    all_to_all x0 -> x3, blocking collectives: none -> 63.2 us  [the longest x2 33.8 us: share(): return lax.all_to_all(stacked, axes, 0, 0, tiled=True)]
    psum x1 -> x0, waiting for transfers between devices: 40.7 us -> none  [on_device(): mixed_full = lax.psum(summand, 'tp')]
    all_to_all x1 -> x5, waiting for transfers between devices: 19 us -> 49.1 us  [the longest x1 22.6 us: on_device(): lax.all_to_all(produced.reshape(groups * Y, cap, col), ALL, 0, 0, tiled=T...]
    all_to_all x1 -> x5, starting transfers between devices: 6.67 us -> 32 us  [the longest x2 10.7 us: share(): return lax.all_to_all(stacked, axes, 0, 0, tiled=True)]
    unnamed x5 -> x0, waiting for transfers between devices: 20.3 us -> none
  transfers between devices with their start and end apart: 5 -> 6, of which waited for: 5 -> 6; matrix products, arithmetic and copies ran while one was open for 1% -> 3% of each run, Pallas kernels for 0% -> 0%
where the time goes in v1:
time: 204 us; the launch traced here: 203 us
  blocking collectives  63.2 us (31%)
  waiting for transfers between devices  51.8 us (25%)
  starting transfers between devices  35.9 us (18%)
  local copies, waits for them, and re-layouts  19.9 us (10%)
  matrix products  18.5 us (9%)
  other arithmetic  12.8 us (6%)
    all_to_all x2, blocking collectives, share(): return lax.all_to_all(stacked, axes, 0, 0, tiled=True)  33.8 us
    all_to_all x1, blocking collectives, on_device(): lax.all_to_all(sent.reshape(groups, cap, width), REQ, 0, 0, tiled=True)  29.3 us
    all_to_all x1, waiting for transfers between devices, on_device(): lax.all_to_all(produced.reshape(groups * Y, cap, col), ALL, 0, 0, tiled=T...  22.6 us
    all_to_all x2, starting transfers between devices, share(): return lax.all_to_all(stacked, axes, 0, 0, tiled=True)  10.7 us
    all_to_all x1, waiting for transfers between devices, on_device(): tops = lax.all_to_all(tops.reshape(groups * Y, rows), ALL, 0, 0, tiled=True)  10.1 us
    all_to_all x2, waiting for transfers between devices, share(): return lax.all_to_all(stacked, axes, 0, 0, tiled=True)  8.56 us
    all_to_all x1, starting transfers between devices, on_device(): lax.all_to_all(produced.reshape(groups * Y, cap, col), ALL, 0, 0, tiled=T...  7.88 us
    all_to_all x1, waiting for transfers between devices, on_device(): lax.all_to_all(outgoing.reshape(Z, rows, -1), 'z', 0, 0, tiled=True)  7.83 us
  transfers between devices with their start and end apart: 6, of which 6 were waited for; matrix products, arithmetic and copies ran while one was open for 3% of the time, Pallas kernels for 0%

profile of v1, /device:TPU:1, one launch (start us, length us, event | category | flops | bytes accessed | tf_op | source)
XLA Modules:
  0.0 202.9 jit_solution(13689042986806660643)
XLA Ops:
  2.2 6.5 %all-to-all-start = ((bf16[8,8,1536]{2,1,0:T(8,128)(2,1)}), bf16[8,8,1536]{2,1,0:T(8,128)(2,1)S(1)}, u32[]{:S(2)}, u32[]{:S(2)}) async-start(bf16[8,8,1536]{2,1,0:T(8,128)(2,1)} %broadcast_in_dim.67), calls=%async_computation | async-start | bytes 393216 | tf_op jit(solution)/shard_map/all_to_all | solution.py:47
  9.8 4.9 %all-to-all-done = bf16[8,8,1536]{2,1,0:T(8,128)(2,1)S(1)} async-done(((bf16[8,8,1536]{2,1,0:T(8,128)(2,1)}), bf16[8,8,1536]{2,1,0:T(8,128)(2,1)S(1)}, u32[]{:S(2)}, u32[]{:S(2)}) %all-to-all-start) | async-done | bytes 196640 | tf_op jit(solution)/shard_map/all_to_all | solution.py:47
  15.6 7.4 %all-to-all-start.1 = ((bf16[8,8,1536]{2,1,0:T(8,128)(2,1)}), bf16[8,8,1536]{2,1,0:T(8,128)(2,1)S(1)}, u32[]{:S(2)}, u32[]{:S(2)}) async-start(bf16[8,8,1536]{2,1,0:T(8,128)(2,1)} %fusion), calls=%async_computation.1 | async-start | bytes 393216 | tf_op jit(solution)/shard_map/all_to_all | solution.py:87
  23.7 7.8 %all-to-all-done.1 = bf16[8,8,1536]{2,1,0:T(8,128)(2,1)S(1)} async-done(((bf16[8,8,1536]{2,1,0:T(8,128)(2,1)}), bf16[8,8,1536]{2,1,0:T(8,128)(2,1)S(1)}, u32[]{:S(2)}, u32[]{:S(2)}) %all-to-all-start.1) | async-done | bytes 196640 | tf_op jit(solution)/shard_map/all_to_all | solution.py:87
  36.4 4.2 %all-to-all-start.2 = ((bf16[4,8,3200]{2,1,0:T(8,128)(2,1)}), bf16[4,8,3200]{2,1,0:T(8,128)(2,1)S(1)}, u32[]{:S(2)}, u32[]{:S(2)}) async-start(bf16[4,8,3200]{2,1,0:T(8,128)(2,1)} %broadcast_in_dim.70), calls=%async_computation.2 | async-start | bytes 409600 | tf_op jit(solution)/shard_map/all_to_all | solution.py:47
  42.1 3.7 %all-to-all-done.2 = bf16[4,8,3200]{2,1,0:T(8,128)(2,1)S(1)} async-done(((bf16[4,8,3200]{2,1,0:T(8,128)(2,1)}), bf16[4,8,3200]{2,1,0:T(8,128)(2,1)S(1)}, u32[]{:S(2)}, u32[]{:S(2)}) %all-to-all-start.2) | async-done | bytes 204832 | tf_op jit(solution)/shard_map/all_to_all | solution.py:47
  48.6 2.6 %reshape.355 = bf16[64,2,2560]{2,1,0:T(2,128)(2,1)} reshape(bf16[128,2560]{1,0:T(8,128)(2,1)} %convolution_convert_fusion) | data formatting | bytes 1310720 | tf_op jit(solution)/shard_map/reshape | solution.py:115
  51.2 29.3 %all_to_all.44 = bf16[64,2,2560]{2,1,0:T(2,128)(2,1)} all-to-all(bf16[64,2,2560]{2,1,0:T(2,128)(2,1)} %reshape.355), channel_id=1, replica_groups=mesh['x'=4,'z'=8,'c'=2,'y'=4] {'x','z','c'}, dimensions={0} | all-to-all | bytes 1310720 | tf_op jit(solution)/shard_map/all_to_all | solution.py:115
  80.5 2.7 %reshape.356 = bf16[128,2560]{1,0:T(8,128)(2,1)} reshape(bf16[64,2,2560]{2,1,0:T(2,128)(2,1)} %all_to_all.44) | data formatting | bytes 1310720 | tf_op jit(solution)/shard_map/reshape | solution.py:116
  83.3 2.3 %fusion.4 = f32[128,384]{1,0:T(8,128)S(1)} fusion(bf16[128,2560]{1,0:T(8,128)(2,1)} %reshape.356, bf16[1,2,2560,384]{3,2,1,0:T(8,128)(2,1)} %param.24), kind=kOutput, calls=%fused_computation.16 | convolution fusion | flops 251658240 | bytes 2818048 | tf_op jit(solution)/shard_map/dot_general | solution.py:117
  85.5 4.1 %convolution_convert_fusion.1 = bf16[128,2560]{1,0:T(8,128)(2,1)} fusion(bf16[1,384,2560]{2,1,0:T(8,128)(2,1)} %param.25, bf16[128,2560]{1,0:T(8,128)(2,1)} %reshape.356, bf16[1,2,2560,384]{3,2,1,0:T(8,128)(2,1)} %param.24, f32[128,384]{1,0:T(8,128)S(1)} %fusion.4), kind=kOutput, calls=%fused_computation.9 | convolution fusion | flops 503939072 | bytes 5439488 | tf_op jit(solution)/shard_map/dot_general | solution.py:120
  89.7 2.4 %reshape.357 = bf16[64,2,4,640]{3,2,1,0:T(4,128)(2,1)} reshape(bf16[128,2560]{1,0:T(8,128)(2,1)} %convolution_convert_fusion.1) | data formatting | bytes 1310720 | tf_op jit(solution)/shard_map/reshape | solution.py:122
  92.0 2.5 %copy.50 = bf16[64,2,4,640]{3,1,2,0:T(2,128)(2,1)} copy(bf16[64,2,4,640]{3,2,1,0:T(4,128)(2,1)} %reshape.357) | data formatting | bytes 1310720 | tf_op jit(solution)/shard_map/reshape | solution.py:122
  94.5 7.9 %all-to-all-start.4 = ((bf16[256,2,640]{2,1,0:T(2,128)(2,1)}), bf16[256,2,640]{2,1,0:T(2,128)(2,1)}, u32[]{:S(2)}, u32[]{:S(2)}) async-start(bf16[256,2,640]{2,1,0:T(2,128)(2,1)} %bitcast.110), calls=%async_computation.4 | async-start | bytes 1310720 | tf_op jit(solution)/shard_map/all_to_all | solution.py:123
  103.1 22.6 %all-to-all-done.4 = bf16[256,2,640]{2,1,0:T(2,128)(2,1)} async-done(((bf16[256,2,640]{2,1,0:T(2,128)(2,1)}), bf16[256,2,640]{2,1,0:T(2,128)(2,1)}, u32[]{:S(2)}, u32[]{:S(2)}) %all-to-all-start.4) | async-done | bytes 655392 | tf_op jit(solution)/shard_map/all_to_all | solution.py:123
  125.7 2.7 %reshape.359 = bf16[512,640]{1,0:T(8,128)(2,1)} reshape(bf16[256,2,640]{2,1,0:T(2,128)(2,1)} %all-to-all-done.4) | data formatting | bytes 1310720 | tf_op jit(solution)/shard_map/reshape | solution.py:125
  130.5 15.7 %all_to_all.45 = bf16[32,8,640]{2,1,0:T(8,128)(2,1)S(1)} all-to-all(bf16[32,8,640]{2,1,0:T(8,128)(2,1)S(1)} %broadcast_in_dim.80), channel_id=1, replica_groups=mesh['x'=4,'z'=8,'c'=2,'y'=4] {'z','y'}, dimensions={0} | all-to-all | bytes 655360 | tf_op jit(solution)/shard_map/all_to_all | solution.py:47
  146.3 18.1 %all_to_all.46 = bf16[4,32,8,640]{3,2,1,0:T(8,128)(2,1)} all-to-all(bf16[4,32,8,640]{3,2,1,0:T(8,128)(2,1)S(1)} %broadcast_in_dim.81), channel_id=1, replica_groups=mesh['x'=4,'z'=8,'c'=2,'y'=4] {'x'}, dimensions={0} | all-to-all | bytes 2621440 | tf_op jit(solution)/shard_map/all_to_all | solution.py:47
  164.5 3.9 %collective-permute-start = (bf16[4,32,8,640]{3,2,1,0:T(8,128)(2,1)}, bf16[4,32,8,640]{3,2,1,0:T(8,128)(2,1)}, u32[]{:S(2)}, u32[]{:S(2)}) collective-permute-start(bf16[4,32,8,640]{3,2,1,0:T(8,128)(2,1)} %all_to_all.46), channel_id=1, source_target_pairs={{0,4},{4,0},{1,5},{5,1},{2,6},{6,2},{3,7},{7,3},{8,12},{12,8},{9,1... | collective-permute-start | bytes 3932168 | tf_op jit(solution)/shard_map/ppermute | solution.py:136
  168.7 2.6 %collective-permute-done = bf16[4,32,8,640]{3,2,1,0:T(8,128)(2,1)} collective-permute-done((bf16[4,32,8,640]{3,2,1,0:T(8,128)(2,1)}, bf16[4,32,8,640]{3,2,1,0:T(8,128)(2,1)}, u32[]{:S(2)}, u32[]{:S(2)}) %collective-permute-start) | collective-permute-done | bytes 1310752 | tf_op jit(solution)/shard_map/ppermute | solution.py:136
  173.3 2.6 %multiply_reduce_fusion.2 = (f32[2,4,8,8]{3,2,1,0:T(8,128)S(1)}, f32[2,4,8,1,8,640]{5,4,3,2,1,0:T(8,128)}, f32[2,4,8,8]{3,2,1,0:T(8,128)S(1)}, f32[2,4,8,1,8,640...) fusion(bf16[1,4,8,4,8,640]{5,4,3,2,1,0:T(8,128)(2,1)S(1)} %bitc, ...), kind=kLoop, calls=%fused_computation.37 | loop fusion | flops 5240832 | bytes 7872512 | tf_op jit(solution)/shard_map/reduce_sum | solution.py:146
  176.9 3.2 %fusion.9 = (bf16[512,640]{1,0:T(8,128)(2,1)S(1)}, bf16[512,640]{1,0:T(8,128)(2,1)S(1)}, bf16[512,640]{1,0:T(8,128)(2,1)S(1)}, bf16[512,640]{1,0:T(8,128)(2,1)S(1)}) fusion(f32[2,4,8,1,8,640]{5,4,3,2,1,0:T(8,128)} %get-tuple-element.16, f32[640]{0:T(1024)S(1)} %get-tuple-element.29, f32[512]{0:T(512)S(1)} %rsqrt.16, f32[640]{0:T(1024)S(1)} %get-tuple-element.30, ...), kind=kLoop, calls=%fused_computation.25 | loop fusion | flops 3932160 | bytes 7876608 | tf_op jit(solution)/shard_map/convert_element_type | solution.py:151
  183.3 6.0 %all-to-all-start.7 = ((f32[256,1,8]{2,1,0:T(1,128)}), f32[256,1,8]{2,1,0:T(1,128)S(1)}, u32[]{:S(2)}, u32[]{:S(2)}) async-start(f32[256,1,8]{2,1,0:T(1,128)} %bitcast.32), calls=%async_computation.7 | async-start | bytes 262144 | tf_op jit(solution)/shard_map/all_to_all | solution.py:162
  192.0 10.1 %all-to-all-done.7 = f32[256,1,8]{2,1,0:T(1,128)S(1)} async-done(((f32[256,1,8]{2,1,0:T(1,128)}), f32[256,1,8]{2,1,0:T(1,128)S(1)}, u32[]{:S(2)}, u32[]{:S(2)}) %all-to-all-start.7) | async-done | bytes 8224 | tf_op jit(solution)/shard_map/all_to_all | solution.py:162
  (96 shorter events, 26.0 us)
Async XLA Ops:
  0.6 34.6 %copy-start = (bf16[640,2560]{1,0:T(8,128)(2,1)S(1)}, bf16[640,2560]{1,0:T(8,128)(2,1)}, u32[]{:S(2)}) copy-start(bf16[640,2560]{1,0:T(8,128)(2,1)} %param.22) | copy-start | bytes 9830404
  0.6 22.4 %copy-start.8 = (s32[8,6]{1,0:T(8,128)S(1)}, s32[8,6]{1,0:T(8,128)}, u32[]{:S(2)}) copy-start(s32[8,6]{1,0:T(8,128)} %param.20) | copy-start | bytes 580
  0.7 22.6 %copy-start.9 = (s32[8]{0:T(128)S(1)}, s32[8]{0:T(128)}, u32[]{:S(2)}) copy-start(s32[8]{0:T(128)} %param.18) | copy-start | bytes 100
  2.2 12.4 %all-to-all-start = ((bf16[8,8,1536]{2,1,0:T(8,128)(2,1)}), bf16[8,8,1536]{2,1,0:T(8,128)(2,1)S(1)}, u32[]{:S(2)}, u32[]{:S(2)}) async-start(bf16[8,8,1536]{2,1,0:T(8,128)(2,1)} %broadcast_in_dim.67), calls=%async_computation | async-start | bytes 393216 | tf_op jit(solution)/shard_map/all_to_all | solution.py:47
  15.6 15.9 %all-to-all-start.1 = ((bf16[8,8,1536]{2,1,0:T(8,128)(2,1)}), bf16[8,8,1536]{2,1,0:T(8,128)(2,1)S(1)}, u32[]{:S(2)}, u32[]{:S(2)}) async-start(bf16[8,8,1536]{2,1,0:T(8,128)(2,1)} %fusion), calls=%async_computation.1 | async-start | bytes 393216 | tf_op jit(solution)/shard_map/all_to_all | solution.py:87
  23.1 0.6 copy-start.3
  36.4 9.4 %all-to-all-start.2 = ((bf16[4,8,3200]{2,1,0:T(8,128)(2,1)}), bf16[4,8,3200]{2,1,0:T(8,128)(2,1)S(1)}, u32[]{:S(2)}, u32[]{:S(2)}) async-start(bf16[4,8,3200]{2,1,0:T(8,128)(2,1)} %broadcast_in_dim.70), calls=%async_computation.2 | async-start | bytes 409600 | tf_op jit(solution)/shard_map/all_to_all | solution.py:47
  46.0 0.6 copy-start.2
  92.0 10.4 %copy-start.6 = (f32[8,6]{1,0:T(8,128)S(1)}, f32[8,6]{1,0:T(8,128)}, u32[]{:S(2)}) copy-start(f32[8,6]{1,0:T(8,128)} %param.21) | copy-start | bytes 580
  92.0 10.7 %copy-start.4 = (s32[8,6]{0,1:T(8,128)S(1)}, s32[8,6]{0,1:T(8,128)}, u32[]{:S(2)}) copy-start(s32[8,6]{0,1:T(8,128)} %copy-done.3) | copy-start | bytes 580
  94.5 31.2 %all-to-all-start.4 = ((bf16[256,2,640]{2,1,0:T(2,128)(2,1)}), bf16[256,2,640]{2,1,0:T(2,128)(2,1)}, u32[]{:S(2)}, u32[]{:S(2)}) async-start(bf16[256,2,640]{2,1,0:T(2,128)(2,1)} %bitcast.110), calls=%async_computation.4 | async-start | bytes 1310720 | tf_op jit(solution)/shard_map/all_to_all | solution.py:123
  146.3 22.3 %copy-start.7 = (s32[512]{0:T(512)S(1)}, s32[512]{0:T(512)}, u32[]{:S(2)}) copy-start(s32[512]{0:T(512)} %param.19) | copy-start | bytes 6148
  146.3 22.4 %copy-start.5 = (f32[2560]{0:T(1024)S(1)}, f32[2560]{0:T(1024)}, u32[]{:S(2)}) copy-start(f32[2560]{0:T(1024)} %param.26) | copy-start | bytes 30724
  164.5 6.9 %collective-permute-start = (bf16[4,32,8,640]{3,2,1,0:T(8,128)(2,1)}, bf16[4,32,8,640]{3,2,1,0:T(8,128)(2,1)}, u32[]{:S(2)}, u32[]{:S(2)}) collective-permute-start(bf16[4,32,8,640]{3,2,1,0:T(8,128)(2,1)} %all_to_all.46), channel_id=1, source_target_pairs={{0,4},{4,0},{1,5},{5,1},{2,6},{6,2},{3,7},{7,3},{8,12},{12,8},{9,1... | collective-permute-start | bytes 3932168 | tf_op jit(solution)/shard_map/ppermute | solution.py:136
  176.9 3.2 %copy-start.1 = (bf16[404,2560]{1,0:T(8,128)(2,1)S(1)}, bf16[404,2560]{1,0:T(8,128)(2,1)}, u32[]{:S(2)}) copy-start(bf16[404,2560]{1,0:T(8,128)(2,1)} %param.27) | copy-start | bytes 6205444
  183.3 18.8 %all-to-all-start.7 = ((f32[256,1,8]{2,1,0:T(1,128)}), f32[256,1,8]{2,1,0:T(1,128)S(1)}, u32[]{:S(2)}, u32[]{:S(2)}) async-start(f32[256,1,8]{2,1,0:T(1,128)} %bitcast.32), calls=%async_computation.7 | async-start | bytes 262144 | tf_op jit(solution)/shard_map/all_to_all | solution.py:162

commit v2 on v1

--- a/solution.py
+++ b/solution.py
@@ -63,11 +63,10 @@
     final_gain,
     vocab_w,
 ):
+    vocab_other = lax.ppermute(vocab_w, "c", [(0, 1), (1, 0)])
     ix, iz, ic, iy = (lax.axis_index(a) for a in ALL)
     rows = queries.shape[0]
     groups = X * Z * C
-    total = groups * rows
-    group_index = (ix * Z + iz) * C + ic
     col = residual.shape[1]
     width = attn_out_w.shape[1]
     kv_width = new_kv.shape[2]
@@ -111,62 +110,90 @@
         jnp.broadcast_to(row_share[:, :, None], (rows, groups, cap)).reshape(rows, -1),
         0.0,
     )
-    sent = jnp.dot(place.T.astype(BF), normed, preferred_element_type=F32).astype(BF)
-    inbound = lax.all_to_all(sent.reshape(groups, cap, width), REQ, 0, 0, tiled=True)
-    inbound = inbound.reshape(groups * cap, width)
+    pairs = groups * cap
+    lines = pairs * Y
+    spread = jnp.repeat(place.astype(BF), Y, axis=1)
+    chunk_of_line = (int_range(lines) % Y)[None, :]
+    spread = jnp.concatenate(
+        [jnp.where(chunk_of_line == t, spread, 0) for t in range(Y)], axis=0
+    )
+    tall = jnp.concatenate([normed[:, t * col : (t + 1) * col] for t in range(Y)], axis=0)
+    sent = lax.dot_general(
+        spread, tall, (((0,), (0,)), ((), ())), preferred_element_type=F32
+    ).astype(BF)
+    inbound = lax.all_to_all(sent.reshape(groups, cap * Y, col), REQ, 0, 0, tiled=True)
+    by_chunk = int_range(lines)
+    by_chunk = by_chunk % pairs * Y + by_chunk // pairs
+    order = (by_chunk[:, None] == int_range(lines)[None, :]).astype(BF)
+    inbound = jnp.dot(order, inbound.reshape(lines, col), preferred_element_type=F32).astype(BF)
+    inbound = jnp.concatenate([inbound[t * pairs : (t + 1) * pairs] for t in range(Y)], axis=1)
     gate_val = jnp.dot(inbound, expert_gate_up[0, 0], preferred_element_type=F32)
     upward = jnp.dot(inbound, expert_gate_up[0, 1], preferred_element_type=F32)
     active = (jax.nn.silu(gate_val) * upward).astype(BF)
     produced = jnp.dot(active, expert_down[0], preferred_element_type=F32).astype(BF)
 
-    produced = produced.reshape(groups, cap, Y, col).transpose(0, 2, 1, 3)
+    produced = jnp.concatenate([produced[:, t * col : (t + 1) * col] for t in range(Y)], axis=0)
+    produced = lax.dot_general(
+        order, produced, (((0,), (0,)), ((), ())), preferred_element_type=F32
+    ).astype(BF)
     returned = lax.all_to_all(
-        produced.reshape(groups * Y, cap, col), ALL, 0, 0, tiled=True
-    ).reshape(groups * Y * cap, col)
-    blend = jnp.broadcast_to(
-        blend.reshape(rows, groups, 1, cap), (rows, groups, Y, cap)
-    ).reshape(rows, -1)
+        produced.reshape(groups, cap * Y, col), REQ, 0, 0, tiled=True
+    ).reshape(lines, col)
+    blend = jnp.repeat(blend, Y, axis=1)
+    blend = jnp.concatenate(
+        [jnp.where(chunk_of_line == t, blend, 0.0) for t in range(Y)], axis=0
+    )
     blend_high = lax.reduce_precision(blend, 8, 7)
     blend_two = jnp.concatenate([blend_high, blend - blend_high], axis=0).astype(BF)
     moe_two = jnp.dot(blend_two, returned, preferred_element_type=F32)
-    state_cols = (mixed_cols + moe_two[:rows] + moe_two[rows:]).astype(BF)
+    moe_part = (moe_two[: Y * rows] + moe_two[Y * rows :]).astype(BF).reshape(Y, rows, col)
+    moe_cols = lax.all_to_all(moe_part, "y", 0, 0, tiled=True)
+    state_cols = (mixed_cols + jnp.sum(moe_cols.astype(F32), axis=0)).astype(BF)
 
     by_zy = share(state_cols, ("z", "y"), Z * Y)
-    by_x = share(by_zy, ("x",), X)
-    other = lax.ppermute(by_x, "c", [(0, 1), (1, 0)])
-    first = jnp.where(ic == 0, by_x, other)
-    second = jnp.where(ic == 0, other, by_x)
-    every = jnp.stack([first, second]).reshape(C, X, Z, Y, rows, col)
-    chunks = [every[:, :, :, t].reshape(total, col) for t in range(Y)]
-    slot_of = (
-        ((int_range(X)[None, :, None] * Z + int_range(Z)[None, None, :]) * C)
-        + int_range(C)[:, None, None]
-    )[..., None] * rows + int_range(rows)
-    slot_of = slot_of.reshape(-1)
+    by_x = share(by_zy, ("x",), X).reshape(X, Z, Y, rows, col)
+    every = by_x.transpose(2, 0, 1, 3, 4)
+    chunks = [by_x[:, :, t].reshape(X * Z * rows, col) for t in range(Y)]
+    half = X * Z * rows
+    slot_of = ((int_range(X)[:, None] * Z + int_range(Z)[None, :]) * C + ic)[..., None]
+    slot_of = (slot_of * rows + int_range(rows)).reshape(-1)
     square = sum(jnp.sum(jnp.square(c.astype(F32)), axis=1) for c in chunks)
     mean_eps = square / width + epsilon
-    row_scale = lax.rsqrt(mean_eps)[:, None]
     logits = 0.0
+    logits_other = 0.0
     for t, c in enumerate(chunks):
-        ready = (c.astype(F32) * row_scale * final_gain[t * col : (t + 1) * col]).astype(BF)
+        gained = (c.astype(F32) * final_gain[t * col : (t + 1) * col]).astype(BF)
+        cut = slice(t * col, (t + 1) * col)
+        meet = (((1,), (1,)), ((), ()))
         logits = logits + lax.dot_general(
-            ready,
-            vocab_w[:, t * col : (t + 1) * col],
-            (((1,), (1,)), ((), ())),
-            preferred_element_type=F32,
+            gained, vocab_w[:, cut], meet, preferred_element_type=F32
         )
-    local_top = jnp.max(logits, axis=1)
+        logits_other = logits_other + lax.dot_general(
+            gained, vocab_other[:, cut], meet, preferred_element_type=F32
+        )
+    local_top = jnp.maximum(jnp.max(logits, axis=1), jnp.max(logits_other, axis=1))
+    local_top = local_top * lax.rsqrt(mean_eps)
     pick = request_perm[:, None] == slot_of[None, :]
-    top_by_request = jnp.sum(jnp.where(pick, local_top[None, :], 0.0), axis=1)
+    top_by_request = jnp.max(jnp.where(pick, local_top[None, :], -jnp.inf), axis=1)
     tops = jnp.broadcast_to(top_by_request.reshape(groups, 1, rows), (groups, Y, rows))
     tops = lax.all_to_all(tops.reshape(groups * Y, rows), ALL, 0, 0, tiled=True)
     top_logit = jnp.max(tops, axis=0)
 
-    wanted = lax.dynamic_slice_in_dim(request_perm, group_index * rows, rows)
+    chip_rows = C * rows
+    wanted = lax.dynamic_slice_in_dim(request_perm, (ix * Z + iz) * chip_rows, chip_rows)
     back = wanted[:, None] == slot_of[None, :]
-    own_chunk = lax.dynamic_index_in_dim(every, iy, 3, keepdims=False).reshape(total, col)
-    hidden_out = jnp.dot(back.astype(BF), own_chunk, preferred_element_type=F32).astype(BF)
-    state_norm = jnp.sqrt(jnp.sum(jnp.where(back, mean_eps[None, :], 0.0), axis=1))
+    own_chunk = lax.dynamic_index_in_dim(every, iy, 0, keepdims=False).reshape(half, col)
+    found = jnp.dot(back.astype(BF), own_chunk, preferred_element_type=F32).astype(BF)
+    found_mean = jnp.sum(jnp.where(back, mean_eps[None, :], 0.0), axis=1)
+    found = found.reshape(C, rows, col)
+    found_mean = found_mean.reshape(C, rows)
+    swap = [(0, 1), (1, 0)]
+    crossed = lax.ppermute(jnp.where(ic == 0, found[1], found[0]), "c", swap)
+    crossed_mean = lax.ppermute(jnp.where(ic == 0, found_mean[1], found_mean[0]), "c", swap)
+    kept = jnp.where(ic == 0, found[0], found[1])
+    kept_mean = jnp.where(ic == 0, found_mean[0], found_mean[1])
+    hidden_out = (kept.astype(F32) + crossed.astype(F32)).astype(BF)
+    state_norm = jnp.sqrt(kept_mean + crossed_mean)
     return (hidden_out, state_norm, top_logit)
 
 

time: 204 us -> 214 us (1.049)
  blocking collectives: 63.2 us -> 15.8 us
  starting transfers between devices: 35.9 us -> 58 us
  waiting for transfers between devices: 51.8 us -> 64.6 us
  matrix products: 18.5 us -> 26.3 us
  other arithmetic: 12.8 us -> 20.5 us
  local copies, waits for them, and re-layouts: 19.9 us -> 25.4 us
    all_to_all x1 -> x0, blocking collectives: 29.3 us -> none  [on_device(): lax.all_to_all(sent.reshape(groups, cap, width), REQ, 0, 0, tiled=True)]
    all_to_all x2 -> x1, blocking collectives: 33.8 us -> 15.8 us  [share(): return lax.all_to_all(stacked, axes, 0, 0, tiled=True)]
    all_to_all x1 -> x3, waiting for transfers between devices: 22.6 us -> 36.7 us  [the longest x1 20.1 us: on_device(): lax.all_to_all(sent.reshape(groups, cap * Y, col), REQ, 0, 0, tiled=True)]
    reshape x6 -> x0, local copies, waits for them, and re-layouts: 13 us -> none  [the longest x2 4.86 us: on_device(): produced = produced.reshape(groups, cap, Y, col).transpose(0, 2, 1, 3)]
    select_n x0 -> x8, local copies, waits for them, and re-layouts: none -> 10.7 us  [the longest x4 5.68 us: on_device(): jnp.where(chunk_of_line == t, spread, 0)]
    all_to_all x1 -> x3, starting transfers between devices: 7.88 us -> 17 us  [the longest x1 6.43 us: on_device(): lax.all_to_all(produced.reshape(groups, cap * Y, col), REQ, 0, 0, tiled=T...]
    dot_general x5 -> x11, matrix products: 4.05 us -> 12.4 us  [the longest x4 5.72 us: on_device(): lax.dot_general(gained, vocab_other[:, cut], meet, preferred_element_type...]
    ppermute x1 -> x3, starting transfers between devices: 3.87 us -> 10.7 us  [the longest x1 5.79 us: on_device(): lax.ppermute(jnp.where(ic == 0, found_mean[1], found_mean[0]), 'c', swap)]
  transfers between devices with their start and end apart: 6 -> 11, of which waited for: 6 -> 6; matrix products, arithmetic and copies ran while one was open for 3% -> 19% of each run, Pallas kernels for 0% -> 0%
where the time goes in v2:
time: 214 us; the launch traced here: 212 us
  waiting for transfers between devices  64.6 us (30%)
  starting transfers between devices  58 us (27%)
  matrix products  26.3 us (12%)
  local copies, waits for them, and re-layouts  25.4 us (12%)
  other arithmetic  20.5 us (10%)
  blocking collectives  15.8 us (7%)
    all_to_all x1, waiting for transfers between devices, on_device(): lax.all_to_all(sent.reshape(groups, cap * Y, col), REQ, 0, 0, tiled=True)  20.1 us
    all_to_all x1, blocking collectives, share(): return lax.all_to_all(stacked, axes, 0, 0, tiled=True)  15.8 us
    all_to_all x3, starting transfers between devices, share(): return lax.all_to_all(stacked, axes, 0, 0, tiled=True)  15.1 us
    all_to_all x1, waiting for transfers between devices, on_device(): lax.all_to_all(produced.reshape(groups, cap * Y, col), REQ, 0, 0, tiled=T...  12.3 us
    all_to_all x1, waiting for transfers between devices, on_device(): tops = lax.all_to_all(tops.reshape(groups * Y, rows), ALL, 0, 0, tiled=True)  11.6 us
    all_to_all x1, waiting for transfers between devices, on_device(): lax.all_to_all(outgoing.reshape(Z, rows, -1), 'z', 0, 0, tiled=True)  8.19 us
    all_to_all x3, waiting for transfers between devices, share(): return lax.all_to_all(stacked, axes, 0, 0, tiled=True)  8.17 us
    all_to_all x1, starting transfers between devices, on_device(): tops = lax.all_to_all(tops.reshape(groups * Y, rows), ALL, 0, 0, tiled=True)  7.73 us
  transfers between devices with their start and end apart: 11, of which 6 were waited for; matrix products, arithmetic and copies ran while one was open for 19% of the time, Pallas kernels for 0%

profile of v2, /device:TPU:1, one launch (start us, length us, event | category | flops | bytes accessed | tf_op | source)
XLA Modules:
  0.0 211.7 jit_solution(16942722280431099679)
XLA Ops:
  2.2 6.5 %all-to-all-start = ((bf16[8,8,1536]{2,1,0:T(8,128)(2,1)}), bf16[8,8,1536]{2,1,0:T(8,128)(2,1)S(1)}, u32[]{:S(2)}, u32[]{:S(2)}) async-start(bf16[8,8,1536]{2,1,0:T(8,128)(2,1)} %broadcast_in_dim.195), calls=%async_computation | async-start | bytes 393216 | tf_op jit(solution)/shard_map/all_to_all | solution.py:47
  18.4 7.5 %all-to-all-start.1 = ((bf16[8,8,1536]{2,1,0:T(8,128)(2,1)}), bf16[8,8,1536]{2,1,0:T(8,128)(2,1)S(1)}, u32[]{:S(2)}, u32[]{:S(2)}) async-start(bf16[8,8,1536]{2,1,0:T(8,128)(2,1)} %fusion), calls=%async_computation.1 | async-start | bytes 393216 | tf_op jit(solution)/shard_map/all_to_all | solution.py:86
  28.5 8.2 %all-to-all-done.1 = bf16[8,8,1536]{2,1,0:T(8,128)(2,1)S(1)} async-done(((bf16[8,8,1536]{2,1,0:T(8,128)(2,1)}), bf16[8,8,1536]{2,1,0:T(8,128)(2,1)S(1)}, u32[]{:S(2)}, u32[]{:S(2)}) %all-to-all-start.1) | async-done | bytes 196640 | tf_op jit(solution)/shard_map/all_to_all | solution.py:86
  38.8 1.7 fusion.133
  43.5 4.2 %all-to-all-start.2 = ((bf16[4,8,3200]{2,1,0:T(8,128)(2,1)}), bf16[4,8,3200]{2,1,0:T(8,128)(2,1)S(1)}, u32[]{:S(2)}, u32[]{:S(2)}) async-start(bf16[4,8,3200]{2,1,0:T(8,128)(2,1)} %broadcast_in_dim.198), calls=%async_computation.2 | async-start | bytes 409600 | tf_op jit(solution)/shard_map/all_to_all | solution.py:47
  48.5 1.8 broadcast_select_fusion.7
  57.6 1.9 fusion.9
  59.5 6.1 %all-to-all-start.3 = ((bf16[64,8,640]{2,1,0:T(8,128)(2,1)}), bf16[64,8,640]{2,1,0:T(8,128)(2,1)}, u32[]{:S(2)}, u32[]{:S(2)}) async-start(bf16[64,8,640]{2,1,0:T(8,128)(2,1)} %fusion.9), calls=%async_computation.3 | async-start | bytes 1310720 | tf_op jit(solution)/shard_map/all_to_all | solution.py:124
  65.6 20.1 %all-to-all-done.3 = bf16[64,8,640]{2,1,0:T(8,128)(2,1)} async-done(((bf16[64,8,640]{2,1,0:T(8,128)(2,1)}), bf16[64,8,640]{2,1,0:T(8,128)(2,1)}, u32[]{:S(2)}, u32[]{:S(2)}) %all-to-all-start.3) | async-done | bytes 655392 | tf_op jit(solution)/shard_map/all_to_all | solution.py:124
  85.7 1.7 convolution_convert_fusion.4
  88.3 2.7 %fusion.4 = f32[128,384]{1,0:T(8,128)} fusion(bf16[1,2,2560,384]{3,2,1,0:T(8,128)(2,1)} %param.24, bf16[128,640]{1,0:T(8,128)(2,1)S(1)} %get-tuple-element.21, bf16[128,640]{1,0:T(8,128)(2,1)S(1)} %get-tuple-element.22, bf16[128,640]{1,0:T(8,128)(2,1)S(1)} %get-tuple-element.23, bf16[128,640]{1,0:T(8,128)(2,1)S(1)} %get-tuple-element.20), kind=kOutput, calls=%fused_computation.7 | convolution fusion | flops 254279680 | bytes 2818048 | tf_op jit(solution)/shard_map/dot_general | solution.py:130
  91.0 4.2 %convolution_convert_fusion = bf16[128,2560]{1,0:T(8,128)(2,1)} fusion(bf16[1,384,2560]{2,1,0:T(8,128)(2,1)} %param.25, bf16[1,2,2560,384]{3,2,1,0:T(8,128)(2,1)} %param.24, f32[128,384]{1,0:T(8,128)} %fusion.4, bf16[128,640]{1,0:T(8,128)(2,1)} %copy-done.3, bf16[128,640]{1,0:T(8,128)(2,1)} %copy-done.4, bf16[128,640]{1,0:T(8,128)(2,1)} %copy-done.5, ...), kind=kOutput, calls=%fused_computation | convolution fusion | flops 506560512 | bytes 5439488 | tf_op jit(solution)/shard_map/dot_general | solution.py:133
  98.0 6.4 %all-to-all-start.4 = ((bf16[64,8,640]{2,1,0:T(8,128)(2,1)}), bf16[64,8,640]{2,1,0:T(8,128)(2,1)}, u32[]{:S(2)}, u32[]{:S(2)}) async-start(bf16[64,8,640]{2,1,0:T(8,128)(2,1)} %fusion.8), calls=%async_computation.4 | async-start | bytes 1310720 | tf_op jit(solution)/shard_map/all_to_all | solution.py:139
  104.6 1.9 broadcast_select_fusion.3
  112.3 12.3 %all-to-all-done.4 = bf16[64,8,640]{2,1,0:T(8,128)(2,1)} async-done(((bf16[64,8,640]{2,1,0:T(8,128)(2,1)}), bf16[64,8,640]{2,1,0:T(8,128)(2,1)}, u32[]{:S(2)}, u32[]{:S(2)}) %all-to-all-start.4) | async-done | bytes 655392 | tf_op jit(solution)/shard_map/all_to_all | solution.py:139
  126.5 4.5 %all-to-all-start.5 = ((bf16[4,8,640]{2,1,0:T(8,128)(2,1)}), bf16[4,8,640]{2,1,0:T(8,128)(2,1)S(1)}, u32[]{:S(2)}, u32[]{:S(2)}) async-start(bf16[4,8,640]{2,1,0:T(8,128)(2,1)} %fusion.72), calls=%async_computation.5 | async-start | bytes 81920 | tf_op jit(solution)/shard_map/all_to_all | solution.py:150
  131.0 4.3 %all-to-all-done.5 = bf16[4,8,640]{2,1,0:T(8,128)(2,1)S(1)} async-done(((bf16[4,8,640]{2,1,0:T(8,128)(2,1)}), bf16[4,8,640]{2,1,0:T(8,128)(2,1)S(1)}, u32[]{:S(2)}, u32[]{:S(2)}) %all-to-all-start.5) | async-done | bytes 40992 | tf_op jit(solution)/shard_map/all_to_all | solution.py:150
  136.1 15.8 %all_to_all.49 = bf16[32,8,640]{2,1,0:T(8,128)(2,1)S(1)} all-to-all(bf16[32,8,640]{2,1,0:T(8,128)(2,1)S(1)} %broadcast_in_dim.211), channel_id=1, replica_groups=mesh['x'=4,'z'=8,'c'=2,'y'=4] {'z','y'}, dimensions={0} | all-to-all | bytes 655360 | tf_op jit(solution)/shard_map/all_to_all | solution.py:47
  153.1 4.3 %all-to-all-start.7 = ((bf16[4,32,8,640]{3,2,1,0:T(8,128)(2,1)}), bf16[4,32,8,640]{3,2,1,0:T(8,128)(2,1)}, u32[]{:S(2)}, u32[]{:S(2)}) async-start(bf16[4,32,8,640]{3,2,1,0:T(8,128)(2,1)} %broadcast_in_dim.212), calls=%async_computation.7 | async-start | bytes 2621440 | tf_op jit(solution)/shard_map/all_to_all | solution.py:47
  157.4 4.6 %collective-permute-start.2 = (bf16[404,2560]{1,0:T(8,128)(2,1)}, bf16[404,2560]{1,0:T(8,128)(2,1)}, u32[]{:S(2)}, u32[]{:S(2)}) collective-permute-start(bf16[404,2560]{1,0:T(8,128)(2,1)} %param.27), channel_id=1, source_target_pairs={{0,4},{4,0},{1,5},{5,1},{2,6},{6,2},{3,7},{7,3},{8,12},{12,8},{9,1... | collective-permute-start | bytes 6205448 | tf_op jit(solution)/shard_map/ppermute | solution.py:66
  162.4 8.2 %all-to-all-done.7 = bf16[4,32,8,640]{3,2,1,0:T(8,128)(2,1)} async-done(((bf16[4,32,8,640]{3,2,1,0:T(8,128)(2,1)}), bf16[4,32,8,640]{3,2,1,0:T(8,128)(2,1)}, u32[]{:S(2)}, u32[]{:S(2)}) %all-to-all-start.7) | async-done | bytes 1310752 | tf_op jit(solution)/shard_map/all_to_all | solution.py:47
  172.6 5.8 %collective-permute-start.1 = (f32[8]{0:T(128)S(1)}, f32[8]{0:T(128)S(1)}, u32[]{:S(2)}, u32[]{:S(2)}) collective-permute-start(f32[8]{0:T(128)S(1)} %broadcast_select_fusion.10), channel_id=1, source_target_pairs={{0,4},{4,0},{1,5},{5,1},{2,6},{6,2},{3,7},{7,3},{8,12},{12,8},{9,1... | collective-permute-start | bytes 104 | tf_op jit(solution)/shard_map/ppermute | solution.py:192
  190.3 7.7 %all-to-all-start.8 = ((f32[256,1,8]{2,1,0:T(1,128)}), f32[256,1,8]{2,1,0:T(1,128)S(1)}, u32[]{:S(2)}, u32[]{:S(2)}) async-start(f32[256,1,8]{2,1,0:T(1,128)} %bitcast.36), calls=%async_computation.8 | async-start | bytes 262144 | tf_op jit(solution)/shard_map/all_to_all | solution.py:179
  199.3 11.6 %all-to-all-done.8 = f32[256,1,8]{2,1,0:T(1,128)S(1)} async-done(((f32[256,1,8]{2,1,0:T(1,128)}), f32[256,1,8]{2,1,0:T(1,128)S(1)}, u32[]{:S(2)}, u32[]{:S(2)}) %all-to-all-start.8) | async-done | bytes 8224 | tf_op jit(solution)/shard_map/all_to_all | solution.py:179
  (134 shorter events, 56.5 us)
Async XLA Ops:
  0.6 41.6 %copy-start = (bf16[640,2560]{1,0:T(8,128)(2,1)S(1)}, bf16[640,2560]{1,0:T(8,128)(2,1)}, u32[]{:S(2)}) copy-start(bf16[640,2560]{1,0:T(8,128)(2,1)} %param.22) | copy-start | bytes 9830404
  2.2 14.6 %all-to-all-start = ((bf16[8,8,1536]{2,1,0:T(8,128)(2,1)}), bf16[8,8,1536]{2,1,0:T(8,128)(2,1)S(1)}, u32[]{:S(2)}, u32[]{:S(2)}) async-start(bf16[8,8,1536]{2,1,0:T(8,128)(2,1)} %broadcast_in_dim.195), calls=%async_computation | async-start | bytes 393216 | tf_op jit(solution)/shard_map/all_to_all | solution.py:47
  18.4 18.3 %all-to-all-start.1 = ((bf16[8,8,1536]{2,1,0:T(8,128)(2,1)}), bf16[8,8,1536]{2,1,0:T(8,128)(2,1)S(1)}, u32[]{:S(2)}, u32[]{:S(2)}) async-start(bf16[8,8,1536]{2,1,0:T(8,128)(2,1)} %fusion), calls=%async_computation.1 | async-start | bytes 393216 | tf_op jit(solution)/shard_map/all_to_all | solution.py:86
  25.9 22.6 %copy-start.8 = (pred[512]{0:T(512)(128)(4,1)}, pred[512]{0:T(512)(128)(4,1)S(1)}, u32[]{:S(2)}) copy-start(pred[512]{0:T(512)(128)(4,1)S(1)} %get-tuple-element.56) | copy-start | bytes 1540
  25.9 22.6 %copy-start.10 = (pred[512]{0:T(512)(128)(4,1)}, pred[512]{0:T(512)(128)(4,1)S(1)}, u32[]{:S(2)}) copy-start(pred[512]{0:T(512)(128)(4,1)S(1)} %get-tuple-element.57) | copy-start | bytes 1540
  43.5 12.5 %all-to-all-start.2 = ((bf16[4,8,3200]{2,1,0:T(8,128)(2,1)}), bf16[4,8,3200]{2,1,0:T(8,128)(2,1)S(1)}, u32[]{:S(2)}, u32[]{:S(2)}) async-start(bf16[4,8,3200]{2,1,0:T(8,128)(2,1)} %broadcast_in_dim.198), calls=%async_computation.2 | async-start | bytes 409600 | tf_op jit(solution)/shard_map/all_to_all | solution.py:47
  56.2 0.6 copy-start.2
  59.5 26.1 %all-to-all-start.3 = ((bf16[64,8,640]{2,1,0:T(8,128)(2,1)}), bf16[64,8,640]{2,1,0:T(8,128)(2,1)}, u32[]{:S(2)}, u32[]{:S(2)}) async-start(bf16[64,8,640]{2,1,0:T(8,128)(2,1)} %fusion.9), calls=%async_computation.3 | async-start | bytes 1310720 | tf_op jit(solution)/shard_map/all_to_all | solution.py:124
  87.5 0.7 copy-start.3
  87.5 0.7 copy-start.4
  87.5 0.8 copy-start.5
  96.5 8.1 %copy-start.9 = (pred[512]{0:T(512)(128)(4,1)S(1)}, pred[512]{0:T(512)(128)(4,1)}, u32[]{:S(2)}) copy-start(pred[512]{0:T(512)(128)(4,1)} %copy-done.8) | copy-start | bytes 1540
  96.5 8.1 %copy-start.11 = (pred[512]{0:T(512)(128)(4,1)S(1)}, pred[512]{0:T(512)(128)(4,1)}, u32[]{:S(2)}) copy-start(pred[512]{0:T(512)(128)(4,1)} %copy-done.10) | copy-start | bytes 1540
  98.0 26.5 %all-to-all-start.4 = ((bf16[64,8,640]{2,1,0:T(8,128)(2,1)}), bf16[64,8,640]{2,1,0:T(8,128)(2,1)}, u32[]{:S(2)}, u32[]{:S(2)}) async-start(bf16[64,8,640]{2,1,0:T(8,128)(2,1)} %fusion.8), calls=%async_computation.4 | async-start | bytes 1310720 | tf_op jit(solution)/shard_map/all_to_all | solution.py:139
  126.5 8.9 %all-to-all-start.5 = ((bf16[4,8,640]{2,1,0:T(8,128)(2,1)}), bf16[4,8,640]{2,1,0:T(8,128)(2,1)S(1)}, u32[]{:S(2)}, u32[]{:S(2)}) async-start(bf16[4,8,640]{2,1,0:T(8,128)(2,1)} %fusion.72), calls=%async_computation.5 | async-start | bytes 81920 | tf_op jit(solution)/shard_map/all_to_all | solution.py:150
  151.9 10.1 %copy-start.7 = (s32[512]{0:T(512)S(1)}, s32[512]{0:T(512)}, u32[]{:S(2)}) copy-start(s32[512]{0:T(512)} %param.19) | copy-start | bytes 6148
  151.9 10.5 %copy-start.6 = (f32[2560]{0:T(1024)S(1)}, f32[2560]{0:T(1024)}, u32[]{:S(2)}) copy-start(f32[2560]{0:T(1024)} %param.26) | copy-start | bytes 30724
  153.1 17.5 %all-to-all-start.7 = ((bf16[4,32,8,640]{3,2,1,0:T(8,128)(2,1)}), bf16[4,32,8,640]{3,2,1,0:T(8,128)(2,1)}, u32[]{:S(2)}, u32[]{:S(2)}) async-start(bf16[4,32,8,640]{3,2,1,0:T(8,128)(2,1)} %broadcast_in_dim.212), calls=%async_computation.7 | async-start | bytes 2621440 | tf_op jit(solution)/shard_map/all_to_all | solution.py:47
  157.4 26.1 %collective-permute-start.2 = (bf16[404,2560]{1,0:T(8,128)(2,1)}, bf16[404,2560]{1,0:T(8,128)(2,1)}, u32[]{:S(2)}, u32[]{:S(2)}) collective-permute-start(bf16[404,2560]{1,0:T(8,128)(2,1)} %param.27), channel_id=1, source_target_pairs={{0,4},{4,0},{1,5},{5,1},{2,6},{6,2},{3,7},{7,3},{8,12},{12,8},{9,1... | collective-permute-start | bytes 6205448 | tf_op jit(solution)/shard_map/ppermute | solution.py:66
  172.6 25.5 %collective-permute-start.1 = (f32[8]{0:T(128)S(1)}, f32[8]{0:T(128)S(1)}, u32[]{:S(2)}, u32[]{:S(2)}) collective-permute-start(f32[8]{0:T(128)S(1)} %broadcast_select_fusion.10), channel_id=1, source_target_pairs={{0,4},{4,0},{1,5},{5,1},{2,6},{6,2},{3,7},{7,3},{8,12},{12,8},{9,1... | collective-permute-start | bytes 104 | tf_op jit(solution)/shard_map/ppermute | solution.py:192
  180.2 18.5 %collective-permute-start = (bf16[8,640]{1,0:T(8,128)(2,1)S(1)}, bf16[8,640]{1,0:T(8,128)(2,1)S(1)}, u32[]{:S(2)}, u32[]{:S(2)}) collective-permute-start(bf16[8,640]{1,0:T(8,128)(2,1)S(1)} %broadcast_select_fusion.9), channel_id=1, source_target_pairs={{0,4},{4,0},{1,5},{5,1},{2,6},{6,2},{3,7},{7,3},{8,12},{12,8},{9,1... | collective-permute-start | bytes 30728 | tf_op jit(solution)/shard_map/ppermute | solution.py:191
  180.5 1.6 copy-start.1
  190.3 20.5 %all-to-all-start.8 = ((f32[256,1,8]{2,1,0:T(1,128)}), f32[256,1,8]{2,1,0:T(1,128)S(1)}, u32[]{:S(2)}, u32[]{:S(2)}) async-start(f32[256,1,8]{2,1,0:T(1,128)} %bitcast.36), calls=%async_computation.8 | async-start | bytes 262144 | tf_op jit(solution)/shard_map/all_to_all | solution.py:179

commit v3 on v2

v3 whole, which is shorter than its diff:
```python
import jax
import jax.numpy as jnp
from jax import lax
from jax.experimental import pallas as pl
from jax.experimental.pallas import tpu as pltpu
from jax.sharding import Mesh, PartitionSpec as P

epsilon = 1e-05
X, Z, C, Y = 4, 8, 2, 4
REQ = ("x", "z", "c")
ALL = ("x", "z", "c", "y")
BF = jnp.bfloat16
F32 = jnp.float32


def attend(queries, fresh_kv, kv_block, lengths, head_dim):
    slot_count, context, kv_heads, _ = kv_block.shape
    groups = queries.shape[1] // head_dim // kv_heads
    query_heads = queries.reshape(slot_count, kv_heads, groups, head_dim)
    key_part = kv_block[..., :head_dim]
    value_part = kv_block[..., head_dim:]
    score_scale = head_dim ** (-0.5)
    scores = (
        jnp.einsum("skgd,sckd->skgc", query_heads, key_part, preferred_element_type=F32)
        * score_scale
    )
    live_mask = (jnp.arange(context, dtype=jnp.int32)[None, :] < lengths[:, None])[:, None, None, :]
    scores = jnp.where(live_mask, scores, -1e30)
    own_score = (
        jnp.einsum(
            "skgd,skd->skg", query_heads, fresh_kv[..., :head_dim], preferred_element_type=F32
        )
        * score_scale
    )
    highest = jnp.maximum(jnp.max(scores, axis=-1), own_score)
    weights = jnp.where(live_mask, jnp.exp(scores - highest[..., None]), 0.0)
    own_weight = jnp.exp(own_score - highest)
    total_weight = jnp.sum(weights, axis=-1) + own_weight
    own_round = lax.reduce_precision(own_weight, 8, 7)
    mixed_sum = jnp.einsum(
        "skgc,sckd->skgd", weights.astype(BF), value_part, preferred_element_type=F32
    )
    mixed_sum = mixed_sum + own_round[..., None] * fresh_kv[:, :, None, head_dim:].astype(F32)
    return (mixed_sum / total_weight[..., None]).reshape(slot_count, -1).astype(BF)


def share(values, axes, count):
    stacked = jnp.broadcast_to(values[None], (count,) + values.shape)
    return lax.all_to_all(stacked, axes, 0, 0, tiled=True)


def route_kernel(groups, cap, ids_ref, wt_ref, spread_ref, blend_ref):
    rows, top_count = ids_ref.shape
    lines = groups * cap * Y
    line = lax.broadcasted_iota(jnp.int32, (rows, lines), 1)
    expert = line // (cap * Y)
    slot = (line // Y) % cap
    chunk = line % Y
    ids = ids_ref[...]
    weights = wt_ref[...]
    share_of = weights / jnp.sum(weights, axis=1, keepdims=True)
    hit = jnp.zeros((rows, lines), F32)
    share_row = jnp.zeros((rows, lines), F32)
    for j in range(top_count):
        same = ids[:, j : j + 1] == expert
        hit = jnp.where(same, 1.0, hit)
        share_row = jnp.where(same, share_of[:, j : j + 1], share_row)
    earlier = jnp.zeros((1, lines), F32)
    ranks = []
    for r in range(rows):
        ranks.append(earlier)
        earlier = earlier + hit[r : r + 1]
    rank = jnp.concatenate(ranks, axis=0)
    placed = jnp.where(rank == slot.astype(F32), hit, 0.0)
    blend = placed * share_row
    high = blend.astype(BF).astype(F32)
    low = blend - high
    for t in range(Y):
        here = chunk == t
        lo, hi = t * rows, (t + 1) * rows
        spread_ref[lo:hi, :] = jnp.where(here, placed, 0.0)
        blend_ref[lo:hi, :] = jnp.where(here, high, 0.0)
        blend_ref[Y * rows + lo : Y * rows + hi, :] = jnp.where(here, low, 0.0)


def route_tables(expert_ids, route_wt, groups, cap):
    rows = expert_ids.shape[0]
    lines = groups * cap * Y
    return pl.pallas_call(
        lambda *refs: route_kernel(groups, cap, *refs),
        out_shape=(
            jax.ShapeDtypeStruct((Y * rows, lines), F32),
            jax.ShapeDtypeStruct((2 * Y * rows, lines), F32),
        ),
        name="route_tables",
    )(expert_ids, route_wt)


def expert_kernel(in_ref, up_ref, down_ref, out_ref, x_ref, acc_ref):
    step = pl.program_id(0)
    lines, col = in_ref.shape
    pairs = lines // Y

    @pl.when(step == 0)
    def _():
        target = lax.broadcasted_iota(jnp.int32, (lines, lines), 0)
        origin = lax.broadcasted_iota(jnp.int32, (lines, lines), 1)
        order = jnp.where(target % pairs * Y + target // pairs == origin, 1.0, 0.0).astype(BF)
        sorted_rows = jnp.dot(order, in_ref[...], preferred_element_type=F32).astype(BF)
        for t in range(Y):
            x_ref[:, t * col : (t + 1) * col] = sorted_rows[t * pairs : (t + 1) * pairs]
        acc_ref[...] = jnp.zeros_like(acc_ref)

    x = x_ref[...]
    gate_val = jnp.dot(x, up_ref[0, 0], preferred_element_type=F32)
    upward = jnp.dot(x, up_ref[0, 1], preferred_element_type=F32)
    active = (gate_val / (1.0 + jnp.exp(-gate_val)) * upward).astype(BF)
    acc_ref[...] += jnp.dot(active, down_ref[0], preferred_element_type=F32)

    @pl.when(step == pl.num_programs(0) - 1)
    def _():
        target = lax.broadcasted_iota(jnp.int32, (lines, lines), 0)
        origin = lax.broadcasted_iota(jnp.int32, (lines, lines), 1)
        order = jnp.where(origin % pairs * Y + origin // pairs == target, 1.0, 0.0).astype(BF)
        for t in range(Y):
            x_ref[:, t * col : (t + 1) * col] = acc_ref[:, t * col : (t + 1) * col].astype(BF)
        tall = jnp.concatenate([x_ref[:, t * col : (t + 1) * col] for t in range(Y)], axis=0)
        out_ref[...] = jnp.dot(order, tall, preferred_element_type=F32).astype(BF)


def run_expert(inbound, gate_up, down):
    lines, col = inbound.shape
    _, _, width, hidden = gate_up.shape
    block = 128
    return pl.pallas_call(
        expert_kernel,
        grid=(hidden // block,),
        in_specs=[
            pl.BlockSpec((lines, col), lambda i: (0, 0)),
            pl.BlockSpec((1, 2, width, block), lambda i: (0, 0, 0, i)),
            pl.BlockSpec((1, block, width), lambda i: (0, i, 0)),
        ],
        out_specs=pl.BlockSpec((lines, col), lambda i: (0, 0)),
        out_shape=jax.ShapeDtypeStruct((lines, col), BF),
        scratch_shapes=[
            pltpu.VMEM((lines // Y, width), BF),
            pltpu.VMEM((lines // Y, width), F32),
        ],
        name="run_expert",
    )(inbound, gate_up, down)


def on_device(
    queries,
    new_kv,
    residual,
    kv_cache,
    cache_len,
    request_perm,
    expert_ids,
    route_wt,
    attn_out_w,
    post_gain,
    expert_gate_up,
    expert_down,
    final_gain,
    vocab_w,
):
    vocab_other = lax.ppermute(vocab_w, "c", [(0, 1), (1, 0)])
    ix, iz, ic, iy = (lax.axis_index(a) for a in ALL)
    rows = queries.shape[0]
    groups = X * Z * C
    col = residual.shape[1]
    width = attn_out_w.shape[1]
    kv_width = new_kv.shape[2]
    head_dim = kv_width // 2
    cap = 2
    int_range = lambda n: jnp.arange(n, dtype=jnp.int32)

    packed = jnp.concatenate([queries, new_kv.reshape(rows, kv_width), residual], axis=1)
    plane = share(packed, ("x", "c"), X * C).reshape(X * C * rows, -1)
    plane_slots = lax.dynamic_index_in_dim(
        request_perm.reshape(X, Z, C * rows), iz, 1, keepdims=False
    ).reshape(-1)
    wanted_slots = (((ix * Z + int_range(Z)) * C + ic) * rows)[:, None] + int_range(rows)[None, :]
    select = (wanted_slots.reshape(-1)[:, None] == plane_slots[None, :]).astype(BF)
    outgoing = jnp.dot(select, plane, preferred_element_type=F32).astype(BF)
    arrived = lax.all_to_all(outgoing.reshape(Z, rows, -1), "z", 0, 0, tiled=True)
    mine = jnp.sum(arrived.astype(F32), axis=0).astype(BF)
    mine_q = mine[:, :col]
    mine_kv = mine[:, col : col + kv_width].reshape(rows, 1, kv_width)
    mine_res = mine[:, col + kv_width :]

    attended = attend(mine_q, mine_kv, kv_cache, cache_len, head_dim)
    partial_value = jnp.dot(attended, attn_out_w, preferred_element_type=F32).astype(BF)
    parts = share(jnp.concatenate([partial_value, mine_res], axis=1), "y", Y)
    full_res = jnp.concatenate([parts[t, :, width:] for t in range(Y)], axis=1).astype(F32)
    mixed_full = full_res + jnp.sum(parts[:, :, :width].astype(F32), axis=0)
    scale_rows = lax.rsqrt(jnp.mean(mixed_full * mixed_full, axis=1, keepdims=True) + epsilon)
    normed = (mixed_full * scale_rows * post_gain).astype(BF)

    spread, blend_two = route_tables(expert_ids, route_wt, groups, cap)
    lines = groups * cap * Y
    tall = jnp.concatenate([normed[:, t * col : (t + 1) * col] for t in range(Y)], axis=0)
    sent = lax.dot_general(
        spread.astype(BF), tall, (((0,), (0,)), ((), ())), preferred_element_type=F32
    ).astype(BF)
    inbound = lax.all_to_all(sent.reshape(groups, cap * Y, col), REQ, 0, 0, tiled=True)
    produced = run_expert(inbound.reshape(lines, col), expert_gate_up, expert_down)

    returned = lax.all_to_all(
        produced.reshape(groups, cap * Y, col), REQ, 0, 0, tiled=True
    ).reshape(lines, col)
    moe_two = jnp.dot(blend_two.astype(BF), returned, preferred_element_type=F32)
    moe_part = (moe_two[: Y * rows] + moe_two[Y * rows :]).astype(BF)
    moe_part = jnp.concatenate([moe_part[t * rows : (t + 1) * rows] for t in range(Y)], axis=1)
    moe_full = jnp.sum(share(moe_part, "y", Y).astype(F32), axis=0)
    state = (mixed_full + moe_full).astype(BF)

    half = X * Z * rows
    every = share(share(state, ("z",), Z), ("x",), X).reshape(half, width)
    slot_of = ((int_range(X)[:, None] * Z + int_range(Z)[None, :]) * C + ic)[..., None]
    slot_of = (slot_of * rows + int_range(rows)).reshape(-1)
    gained = (every.astype(F32) * final_gain).astype(BF)
    meet = (((1,), (1,)), ((), ()))
    logits = lax.dot_general(gained, vocab_w, meet, preferred_element_type=F32)
    logits_other = lax.dot_general(gained, vocab_other, meet, preferred_element_type=F32)
    local_top = jnp.maximum(jnp.max(logits, axis=1), jnp.max(logits_other, axis=1))
    pick = request_perm[:, None] == slot_of[None, :]
    top_by_request = jnp.max(jnp.where(pick, local_top[None, :], -jnp.inf), axis=1)
    every, top_by_request = lax.optimization_barrier((every, top_by_request))
    tops = jnp.broadcast_to(top_by_request.reshape(groups, 1, rows), (groups, Y, rows))
    tops = lax.all_to_all(tops.reshape(groups * Y, rows), ALL, 0, 0, tiled=True)

    chip_rows = C * rows
    wanted = lax.dynamic_slice_in_dim(request_perm, (ix * Z + iz) * chip_rows, chip_rows)
    back = wanted[:, None] == slot_of[None, :]
    found = jnp.dot(back.astype(BF), every, preferred_element_type=F32).astype(BF)
    crossed = lax.ppermute(
        jnp.where(ic == 0, found[rows:], found[:rows]), "c", [(0, 1), (1, 0)]
    )
    hidden = jnp.where(ic == 0, found[:rows], found[rows:]).astype(F32) + crossed.astype(F32)
    hidden_out = lax.dynamic_slice_in_dim(hidden, iy * col, col, 1).astype(BF)
    mean_eps = jnp.mean(hidden * hidden, axis=1) + epsilon
    top_logit = jnp.max(tops, axis=0) * lax.rsqrt(mean_eps)
    return (hidden_out, jnp.sqrt(mean_eps), top_logit)


def solution(mesh):
    fine = Mesh(mesh.devices.reshape(X, Z, C, Y), ALL)
    placed = (
        P(REQ, "y"),
        P(REQ, "y", None),
        P(REQ, "y"),
        P(REQ, None, "y", None),
        P(REQ),
        P(),
        P(REQ, None),
        P(REQ, None),
        P("y", None),
        P(),
        P(REQ, None, None, "y"),
        P(REQ, "y", None),
        P(),
        P(ALL, None),
    )
    return jax.shard_map(
        on_device,
        mesh=fine,
        in_specs=placed,
        out_specs=(P(REQ, "y"), P(REQ), P(REQ)),
        check_vma=False,
    )
```

time: 214 us -> 191 us (0.89)
  blocking collectives: 15.8 us -> 70.2 us
  starting transfers between devices: 58 us -> 35.4 us
  local copies, waits for them, and re-layouts: 25.4 us -> 6.52 us
  waiting for transfers between devices: 64.6 us -> 49.2 us
  other arithmetic: 20.5 us -> 5.87 us
  matrix products: 26.3 us -> 13.4 us
  Pallas kernels: 0 us -> 8.35 us
    all_to_all x0 -> x2, blocking collectives: none -> 54.9 us  [the longest x1 28.4 us: on_device(): lax.all_to_all(sent.reshape(groups, cap * Y, col), REQ, 0, 0, tiled=True)]
    all_to_all x3 -> x0, waiting for transfers between devices: 36.7 us -> none  [the longest x1 20.1 us: on_device(): lax.all_to_all(sent.reshape(groups, cap * Y, col), REQ, 0, 0, tiled=True)]
    all_to_all x3 -> x4, waiting for transfers between devices: 8.17 us -> 28.6 us  [share(): return lax.all_to_all(stacked, axes, 0, 0, tiled=True)]
    all_to_all x3 -> x0, starting transfers between devices: 17 us -> none  [the longest x1 6.43 us: on_device(): lax.all_to_all(produced.reshape(groups, cap * Y, col), REQ, 0, 0, tiled=T...]
    dot_general x15 -> x5, matrix products: 20.9 us -> 8.57 us  [the longest x1 2.76 us: on_device(): logits = lax.dot_general(gained, vocab_w, meet, preferred_element_type=F32)]
    select_n x8 -> x0, local copies, waits for them, and re-layouts: 10.7 us -> none  [the longest x4 5.68 us: on_device(): jnp.where(chunk_of_line == t, spread, 0)]
    pallas_call x0 -> x2, Pallas kernels: none -> 8.35 us  [the longest x1 6.81 us: run_expert(): pl.pallas_call(expert_kernel, grid=(hidden // block,), in_specs=[pl.Block...]
    select_n x5 -> x1, other arithmetic: 5.21 us -> 0.63 us  [on_device(): jnp.where(ic == 0, found[rows:], found[:rows])]
  transfers between devices with their start and end apart: 11 -> 8, of which waited for: 6 -> 6; matrix products, arithmetic and copies ran while one was open for 19% -> 4% of each run, Pallas kernels for 0% -> 1%
where the time goes in v3:
time: 191 us; the launch traced here: 190 us
  blocking collectives  70.2 us (37%)
  waiting for transfers between devices  49.2 us (26%)
  starting transfers between devices  35.4 us (19%)
  matrix products  13.4 us (7%)
  Pallas kernels  8.35 us (4%)
  local copies, waits for them, and re-layouts  6.52 us (3%)
  other arithmetic  5.87 us (3%)
    all_to_all x4, waiting for transfers between devices, share(): return lax.all_to_all(stacked, axes, 0, 0, tiled=True)  28.6 us
    all_to_all x1, blocking collectives, on_device(): lax.all_to_all(sent.reshape(groups, cap * Y, col), REQ, 0, 0, tiled=True)  28.4 us
    all_to_all x1, blocking collectives, on_device(): lax.all_to_all(produced.reshape(groups, cap * Y, col), REQ, 0, 0, tiled=T...  26.5 us
    all_to_all x4, starting transfers between devices, share(): return lax.all_to_all(stacked, axes, 0, 0, tiled=True)  19 us
    all_to_all x1, blocking collectives, share(): return lax.all_to_all(stacked, axes, 0, 0, tiled=True)  15.3 us
    all_to_all x1, waiting for transfers between devices, on_device(): tops = lax.all_to_all(tops.reshape(groups * Y, rows), ALL, 0, 0, tiled=True)  12.8 us
    all_to_all x1, waiting for transfers between devices, on_device(): lax.all_to_all(outgoing.reshape(Z, rows, -1), 'z', 0, 0, tiled=True)  7.78 us
    all_to_all x1, starting transfers between devices, on_device(): lax.all_to_all(outgoing.reshape(Z, rows, -1), 'z', 0, 0, tiled=True)  7.43 us
  transfers between devices with their start and end apart: 8, of which 6 were waited for; matrix products, arithmetic and copies ran while one was open for 4% of the time, Pallas kernels for 1%

profile of v3, /device:TPU:1, one launch (start us, length us, event | category | flops | bytes accessed | tf_op | source)
XLA Modules:
  0.0 189.7 jit_solution(10247451598832330542)
XLA Ops:
  2.2 6.5 %all-to-all-start = ((bf16[8,8,1536]{2,1,0:T(8,128)(2,1)}), bf16[8,8,1536]{2,1,0:T(8,128)(2,1)S(1)}, u32[]{:S(2)}, u32[]{:S(2)}) async-start(bf16[8,8,1536]{2,1,0:T(8,128)(2,1)} %broadcast_in_dim.41), calls=%async_computation | async-start | bytes 393216 | tf_op jit(solution)/shard_map/all_to_all | solution.py:49
  9.8 4.9 %all-to-all-done = bf16[8,8,1536]{2,1,0:T(8,128)(2,1)S(1)} async-done(((bf16[8,8,1536]{2,1,0:T(8,128)(2,1)}), bf16[8,8,1536]{2,1,0:T(8,128)(2,1)S(1)}, u32[]{:S(2)}, u32[]{:S(2)}) %all-to-all-start) | async-done | bytes 196640 | tf_op jit(solution)/shard_map/all_to_all | solution.py:49
  15.6 7.4 %all-to-all-start.1 = ((bf16[8,8,1536]{2,1,0:T(8,128)(2,1)}), bf16[8,8,1536]{2,1,0:T(8,128)(2,1)S(1)}, u32[]{:S(2)}, u32[]{:S(2)}) async-start(bf16[8,8,1536]{2,1,0:T(8,128)(2,1)} %fusion), calls=%async_computation.1 | async-start | bytes 393216 | tf_op jit(solution)/shard_map/all_to_all | solution.py:188
  23.7 7.8 %all-to-all-done.1 = bf16[8,8,1536]{2,1,0:T(8,128)(2,1)S(1)} async-done(((bf16[8,8,1536]{2,1,0:T(8,128)(2,1)}), bf16[8,8,1536]{2,1,0:T(8,128)(2,1)S(1)}, u32[]{:S(2)}, u32[]{:S(2)}) %all-to-all-start.1) | async-done | bytes 196640 | tf_op jit(solution)/shard_map/all_to_all | solution.py:188
  31.7 1.7 fusion.45
  33.6 1.5 fusion.5
  36.4 4.2 %all-to-all-start.2 = ((bf16[4,8,3200]{2,1,0:T(8,128)(2,1)}), bf16[4,8,3200]{2,1,0:T(8,128)(2,1)}, u32[]{:S(2)}, u32[]{:S(2)}) async-start(bf16[4,8,3200]{2,1,0:T(8,128)(2,1)} %broadcast_in_dim.44), calls=%async_computation.2 | async-start | bytes 409600 | tf_op jit(solution)/shard_map/all_to_all | solution.py:49
  40.6 1.5 route_tables.1
  42.1 3.8 %all-to-all-done.2 = bf16[4,8,3200]{2,1,0:T(8,128)(2,1)} async-done(((bf16[4,8,3200]{2,1,0:T(8,128)(2,1)}), bf16[4,8,3200]{2,1,0:T(8,128)(2,1)}, u32[]{:S(2)}, u32[]{:S(2)}) %all-to-all-start.2) | async-done | bytes 204832 | tf_op jit(solution)/shard_map/all_to_all | solution.py:49
  47.9 1.2 fusion.1
  49.1 28.4 %all_to_all.49 = bf16[64,8,640]{2,1,0:T(8,128)(2,1)} all-to-all(bf16[64,8,640]{2,1,0:T(8,128)(2,1)S(1)} %fusion.1), channel_id=1, replica_groups=mesh['x'=4,'z'=8,'c'=2,'y'=4] {'x','z','c'}, dimensions={0} | all-to-all | bytes 1310720 | tf_op jit(solution)/shard_map/all_to_all | solution.py:208
  77.5 6.8 %run_expert.1 = bf16[512,640]{1,0:T(8,128)(2,1)} custom-call(bf16[512,640]{1,0:T(8,128)(2,1)} %bitcast.56, bf16[1,2,2560,384]{3,2,1,0:T(8,128)(2,1)} %up_ref.1, bf16[1,384,2560]{2,1,0:T(8,128)(2,1)} %down_ref.1), custom_call_target="tpu_custom_call" | custom-call | tf_op jit(solution)/shard_map/run_expert/pallas_call | solution.py:135
  84.3 26.5 %all_to_all.50 = bf16[64,8,640]{2,1,0:T(8,128)(2,1)S(1)} all-to-all(bf16[64,8,640]{2,1,0:T(8,128)(2,1)} %bitcast.57), channel_id=1, replica_groups=mesh['x'=4,'z'=8,'c'=2,'y'=4] {'x','z','c'}, dimensions={0} | all-to-all | bytes 1310720 | tf_op jit(solution)/shard_map/all_to_all | solution.py:211
  111.8 3.3 %all-to-all-start.5 = ((bf16[4,8,2560]{2,1,0:T(8,128)(2,1)}), bf16[4,8,2560]{2,1,0:T(8,128)(2,1)S(1)}, u32[]{:S(2)}, u32[]{:S(2)}) async-start(bf16[4,8,2560]{2,1,0:T(8,128)(2,1)} %broadcast_in_dim.45), calls=%async_computation.5 | async-start | bytes 327680 | tf_op jit(solution)/shard_map/all_to_all | solution.py:49
  115.5 4.7 %all-to-all-done.5 = bf16[4,8,2560]{2,1,0:T(8,128)(2,1)S(1)} async-done(((bf16[4,8,2560]{2,1,0:T(8,128)(2,1)}), bf16[4,8,2560]{2,1,0:T(8,128)(2,1)S(1)}, u32[]{:S(2)}, u32[]{:S(2)}) %all-to-all-start.5) | async-done | bytes 163872 | tf_op jit(solution)/shard_map/all_to_all | solution.py:49
  121.1 15.3 %all_to_all.51 = bf16[8,8,2560]{2,1,0:T(8,128)(2,1)S(1)} all-to-all(bf16[8,8,2560]{2,1,0:T(8,128)(2,1)S(1)} %broadcast_in_dim.46), channel_id=1, replica_groups=mesh['x'=4,'z'=8,'c'=2,'y'=4] {'z'}, dimensions={0} | all-to-all | bytes 655360 | tf_op jit(solution)/shard_map/all_to_all | solution.py:49
  137.5 4.9 %all-to-all-start.7 = ((bf16[4,8,8,2560]{3,2,1,0:T(8,128)(2,1)}), bf16[4,8,8,2560]{3,2,1,0:T(8,128)(2,1)}, u32[]{:S(2)}, u32[]{:S(2)}) async-start(bf16[4,8,8,2560]{3,2,1,0:T(8,128)(2,1)} %broadcast_in_dim.47), calls=%async_computation.7 | async-start | bytes 2621440 | tf_op jit(solution)/shard_map/all_to_all | solution.py:49
  142.7 15.2 %all-to-all-done.7 = bf16[4,8,8,2560]{3,2,1,0:T(8,128)(2,1)} async-done(((bf16[4,8,8,2560]{3,2,1,0:T(8,128)(2,1)}), bf16[4,8,8,2560]{3,2,1,0:T(8,128)(2,1)}, u32[]{:S(2)}, u32[]{:S(2)}) %all-to-all-start.7) | async-done | bytes 1310752 | tf_op jit(solution)/shard_map/all_to_all | solution.py:49
  158.0 2.8 %convolution_reduce_fusion.1 = f32[256]{0:T(256)S(1)} fusion(bf16[404,2560]{1,0:T(8,128)(2,1)} %param.27, bf16[256,2560]{1,0:T(8,128)(2,1)} %bitcast.22, f32[2560]{0:T(1024)S(1)} %copy-done.6), kind=kOutput, calls=%fused_computation.8 | convolution fusion | flops 531600128 | bytes 3390464 | tf_op jit(solution)/shard_map/dot_general | solution.py:226
  160.8 2.8 %convolution_reduce_fusion = f32[256]{0:T(256)S(1)} fusion(bf16[404,2560]{1,0:T(8,128)(2,1)} %collective-permute-done, bf16[256,2560]{1,0:T(8,128)(2,1)} %bitcast.22, f32[2560]{0:T(1024)S(1)} %copy-done.6), kind=kOutput, calls=%fused_computation.7 | convolution fusion | flops 531600128 | bytes 3390464 | tf_op jit(solution)/shard_map/dot_general | solution.py:227
  163.8 1.6 convolution_convert_fusion
  166.0 3.4 %collective-permute-start.1 = (bf16[8,2560]{1,0:T(8,128)(2,1)}, bf16[8,2560]{1,0:T(8,128)(2,1)S(1)}, u32[]{:S(2)}, u32[]{:S(2)}) collective-permute-start(bf16[8,2560]{1,0:T(8,128)(2,1)} %broadcast_select_fusion), channel_id=1, source_target_pairs={{0,4},{4,0},{1,5},{5,1},{2,6},{6,2},{3,7},{7,3},{8,12},{12,8},{9,1... | collective-permute-start | bytes 122888 | tf_op jit(solution)/shard_map/ppermute | solution.py:239
  170.2 5.1 %all-to-all-start.8 = ((f32[256,1,8]{2,1,0:T(1,128)}), f32[256,1,8]{2,1,0:T(1,128)S(1)}, u32[]{:S(2)}, u32[]{:S(2)}) async-start(f32[256,1,8]{2,1,0:T(1,128)} %bitcast.23), calls=%async_computation.8 | async-start | bytes 262144 | tf_op jit(solution)/shard_map/all_to_all | solution.py:233
  175.4 12.8 %all-to-all-done.8 = f32[256,1,8]{2,1,0:T(1,128)S(1)} async-done(((f32[256,1,8]{2,1,0:T(1,128)}), f32[256,1,8]{2,1,0:T(1,128)S(1)}, u32[]{:S(2)}, u32[]{:S(2)}) %all-to-all-start.8) | async-done | bytes 8224 | tf_op jit(solution)/shard_map/all_to_all | solution.py:233
  (67 shorter events, 14.6 us)
Async XLA Ops:
  0.6 34.5 %copy-start = (bf16[640,2560]{1,0:T(8,128)(2,1)S(1)}, bf16[640,2560]{1,0:T(8,128)(2,1)}, u32[]{:S(2)}) copy-start(bf16[640,2560]{1,0:T(8,128)(2,1)} %param.22) | copy-start | bytes 9830404
  2.2 12.4 %all-to-all-start = ((bf16[8,8,1536]{2,1,0:T(8,128)(2,1)}), bf16[8,8,1536]{2,1,0:T(8,128)(2,1)S(1)}, u32[]{:S(2)}, u32[]{:S(2)}) async-start(bf16[8,8,1536]{2,1,0:T(8,128)(2,1)} %broadcast_in_dim.41), calls=%async_computation | async-start | bytes 393216 | tf_op jit(solution)/shard_map/all_to_all | solution.py:49
  15.6 15.9 %all-to-all-start.1 = ((bf16[8,8,1536]{2,1,0:T(8,128)(2,1)}), bf16[8,8,1536]{2,1,0:T(8,128)(2,1)S(1)}, u32[]{:S(2)}, u32[]{:S(2)}) async-start(bf16[8,8,1536]{2,1,0:T(8,128)(2,1)} %fusion), calls=%async_computation.1 | async-start | bytes 393216 | tf_op jit(solution)/shard_map/all_to_all | solution.py:188
  35.2 12.6 %copy-start.4 = (f32[2560]{0:T(1024)S(1)}, f32[2560]{0:T(1024)}, u32[]{:S(2)}) copy-start(f32[2560]{0:T(1024)} %param.23) | copy-start | bytes 30724
  36.4 9.5 %all-to-all-start.2 = ((bf16[4,8,3200]{2,1,0:T(8,128)(2,1)}), bf16[4,8,3200]{2,1,0:T(8,128)(2,1)}, u32[]{:S(2)}, u32[]{:S(2)}) async-start(bf16[4,8,3200]{2,1,0:T(8,128)(2,1)} %broadcast_in_dim.44), calls=%async_computation.2 | async-start | bytes 409600 | tf_op jit(solution)/shard_map/all_to_all | solution.py:49
  47.6 36.7 %copy-start.1 = (bf16[8,640]{1,0:T(8,128)(2,1)}, bf16[8,640]{1,0:T(8,128)(2,1)S(1)}, u32[]{:S(2)}) copy-start(bf16[8,640]{1,0:T(8,128)(2,1)S(1)} %get-tuple-element.15) | copy-start | bytes 30724
  47.6 36.7 %copy-start.2 = (bf16[8,640]{1,0:T(8,128)(2,1)}, bf16[8,640]{1,0:T(8,128)(2,1)S(1)}, u32[]{:S(2)}) copy-start(bf16[8,640]{1,0:T(8,128)(2,1)S(1)} %get-tuple-element.16) | copy-start | bytes 30724
  77.5 33.3 %copy-start.3 = (f32[64,512]{1,0:T(8,128)S(1)}, f32[64,512]{1,0:T(8,128)}, u32[]{:S(2)}) copy-start(f32[64,512]{1,0:T(8,128)} %get-tuple-element.7) | copy-start | bytes 393220
  111.8 8.5 %all-to-all-start.5 = ((bf16[4,8,2560]{2,1,0:T(8,128)(2,1)}), bf16[4,8,2560]{2,1,0:T(8,128)(2,1)S(1)}, u32[]{:S(2)}, u32[]{:S(2)}) async-start(bf16[4,8,2560]{2,1,0:T(8,128)(2,1)} %broadcast_in_dim.45), calls=%async_computation.5 | async-start | bytes 327680 | tf_op jit(solution)/shard_map/all_to_all | solution.py:49
  115.1 45.6 %collective-permute-start = (bf16[404,2560]{1,0:T(8,128)(2,1)}, bf16[404,2560]{1,0:T(8,128)(2,1)}, u32[]{:S(2)}, u32[]{:S(2)}) collective-permute-start(bf16[404,2560]{1,0:T(8,128)(2,1)} %param.27), channel_id=1, source_target_pairs={{0,4},{4,0},{1,5},{5,1},{2,6},{6,2},{3,7},{7,3},{8,12},{12,8},{9,1... | collective-permute-start | bytes 6205448 | tf_op jit(solution)/shard_map/ppermute | solution.py:169
  136.3 6.3 %copy-start.5 = (s32[512]{0:T(512)S(1)}, s32[512]{0:T(512)}, u32[]{:S(2)}) copy-start(s32[512]{0:T(512)} %param.19) | copy-start | bytes 6148
  136.4 21.6 %copy-start.6 = (f32[2560]{0:T(1024)S(1)}, f32[2560]{0:T(1024)}, u32[]{:S(2)}) copy-start(f32[2560]{0:T(1024)} %param.26) | copy-start | bytes 30724
  137.5 20.5 %all-to-all-start.7 = ((bf16[4,8,8,2560]{3,2,1,0:T(8,128)(2,1)}), bf16[4,8,8,2560]{3,2,1,0:T(8,128)(2,1)}, u32[]{:S(2)}, u32[]{:S(2)}) async-start(bf16[4,8,8,2560]{3,2,1,0:T(8,128)(2,1)} %broadcast_in_dim.47), calls=%async_computation.7 | async-start | bytes 2621440 | tf_op jit(solution)/shard_map/all_to_all | solution.py:49
  166.0 22.4 %collective-permute-start.1 = (bf16[8,2560]{1,0:T(8,128)(2,1)}, bf16[8,2560]{1,0:T(8,128)(2,1)S(1)}, u32[]{:S(2)}, u32[]{:S(2)}) collective-permute-start(bf16[8,2560]{1,0:T(8,128)(2,1)} %broadcast_select_fusion), channel_id=1, source_target_pairs={{0,4},{4,0},{1,5},{5,1},{2,6},{6,2},{3,7},{7,3},{8,12},{12,8},{9,1... | collective-permute-start | bytes 122888 | tf_op jit(solution)/shard_map/ppermute | solution.py:239
  170.2 18.0 %all-to-all-start.8 = ((f32[256,1,8]{2,1,0:T(1,128)}), f32[256,1,8]{2,1,0:T(1,128)S(1)}, u32[]{:S(2)}, u32[]{:S(2)}) async-start(f32[256,1,8]{2,1,0:T(1,128)} %bitcast.23), calls=%async_computation.8 | async-start | bytes 262144 | tf_op jit(solution)/shard_map/all_to_all | solution.py:233

commit v4 on v3

--- a/solution.py
+++ b/solution.py
@@ -96,55 +96,93 @@
     )(expert_ids, route_wt)
 
 
-def expert_kernel(in_ref, up_ref, down_ref, out_ref, x_ref, acc_ref):
-    step = pl.program_id(0)
-    lines, col = in_ref.shape
+def mix_kernel(parts_ref, gain_ref, spread_ref, mixed_ref, sent_ref):
+    width = gain_ref.shape[1]
+    col = width // Y
+    total = parts_ref[0, :, :width].astype(F32)
+    for t in range(1, Y):
+        total = total + parts_ref[t, :, :width].astype(F32)
+    pieces = [
+        total[:, t * col : (t + 1) * col] + parts_ref[t, :, width:].astype(F32)
+        for t in range(Y)
+    ]
+    square = sum(jnp.sum(p * p, axis=1, keepdims=True) for p in pieces)
+    scale = lax.rsqrt(square / width + epsilon)
+    tall = []
+    for t, p in enumerate(pieces):
+        mixed_ref[:, t * col : (t + 1) * col] = p
+        tall.append(p * scale * gain_ref[:, t * col : (t + 1) * col])
+    tall = jnp.concatenate(tall, axis=0).astype(BF)
+    sent_ref[...] = lax.dot_general(
+        spread_ref[...].astype(BF), tall, (((0,), (0,)), ((), ())), preferred_element_type=F32
+    ).astype(BF)
+
+
+def mix_rows(parts, gain, spread):
+    rows = parts.shape[1]
+    width = gain.shape[0]
+    lines = spread.shape[1]
+    return pl.pallas_call(
+        mix_kernel,
+        out_shape=(
+            jax.ShapeDtypeStruct((rows, width), F32),
+            jax.ShapeDtypeStruct((lines, width // Y), BF),
+        ),
+        name="mix_rows",
+    )(parts, gain.reshape(1, width), spread)
+
+
+def expert_kernel(in_hbm, up_hbm, down_hbm, out_ref, rows_ref, up_ref, down_ref, x_ref, sems):
+    lines, col = rows_ref.shape
     pairs = lines // Y
-
-    @pl.when(step == 0)
-    def _():
-        target = lax.broadcasted_iota(jnp.int32, (lines, lines), 0)
-        origin = lax.broadcasted_iota(jnp.int32, (lines, lines), 1)
-        order = jnp.where(target % pairs * Y + target // pairs == origin, 1.0, 0.0).astype(BF)
-        sorted_rows = jnp.dot(order, in_ref[...], preferred_element_type=F32).astype(BF)
-        for t in range(Y):
-            x_ref[:, t * col : (t + 1) * col] = sorted_rows[t * pairs : (t + 1) * pairs]
-        acc_ref[...] = jnp.zeros_like(acc_ref)
-
-    x = x_ref[...]
-    gate_val = jnp.dot(x, up_ref[0, 0], preferred_element_type=F32)
-    upward = jnp.dot(x, up_ref[0, 1], preferred_element_type=F32)
+    rows_copy = pltpu.make_async_copy(in_hbm, rows_ref, sems.at[0])
+    gate_copy = pltpu.make_async_copy(up_hbm.at[0, 0], up_ref.at[0], sems.at[1])
+    up_copy = pltpu.make_async_copy(up_hbm.at[0, 1], up_ref.at[1], sems.at[2])
+    down_copy = pltpu.make_async_copy(down_hbm.at[0], down_ref, sems.at[3])
+    rows_copy.start()
+    gate_copy.start()
+    up_copy.start()
+    down_copy.start()
+
+    target = lax.broadcasted_iota(jnp.int32, (lines, lines), 0)
+    origin = lax.broadcasted_iota(jnp.int32, (lines, lines), 1)
+    order = jnp.where(target % pairs * Y + target // pairs == origin, 1.0, 0.0).astype(BF)
+    rows_copy.wait()
+    sorted_rows = jnp.dot(order, rows_ref[...], preferred_element_type=F32).astype(BF)
+    for t in range(Y):
+        x_ref[:, t * col : (t + 1) * col] = sorted_rows[t * pairs : (t + 1) * pairs]
+    gate_copy.wait()
+    gate_val = jnp.dot(x_ref[...], up_ref[0], preferred_element_type=F32)
+    up_copy.wait()
+    upward = jnp.dot(x_ref[...], up_ref[1], preferred_element_type=F32)
     active = (gate_val / (1.0 + jnp.exp(-gate_val)) * upward).astype(BF)
-    acc_ref[...] += jnp.dot(active, down_ref[0], preferred_element_type=F32)
-
-    @pl.when(step == pl.num_programs(0) - 1)
-    def _():
-        target = lax.broadcasted_iota(jnp.int32, (lines, lines), 0)
-        origin = lax.broadcasted_iota(jnp.int32, (lines, lines), 1)
-        order = jnp.where(origin % pairs * Y + origin // pairs == target, 1.0, 0.0).astype(BF)
-        for t in range(Y):
-            x_ref[:, t * col : (t + 1) * col] = acc_ref[:, t * col : (t + 1) * col].astype(BF)
-        tall = jnp.concatenate([x_ref[:, t * col : (t + 1) * col] for t in range(Y)], axis=0)
-        out_ref[...] = jnp.dot(order, tall, preferred_element_type=F32).astype(BF)
+    back = jnp.where(origin % pairs * Y + origin // pairs == target, 1.0, 0.0).astype(BF)
+    down_copy.wait()
+    tall = jnp.concatenate(
+        [
+            jnp.dot(
+                active, down_ref[:, t * col : (t + 1) * col], preferred_element_type=F32
+            ).astype(BF)
+            for t in range(Y)
+        ],
+        axis=0,
+    )
+    out_ref[...] = jnp.dot(back, tall, preferred_element_type=F32).astype(BF)
 
 
 def run_expert(inbound, gate_up, down):
     lines, col = inbound.shape
     _, _, width, hidden = gate_up.shape
-    block = 128
     return pl.pallas_call(
         expert_kernel,
-        grid=(hidden // block,),
-        in_specs=[
-            pl.BlockSpec((lines, col), lambda i: (0, 0)),
-            pl.BlockSpec((1, 2, width, block), lambda i: (0, 0, 0, i)),
-            pl.BlockSpec((1, block, width), lambda i: (0, i, 0)),
-        ],
-        out_specs=pl.BlockSpec((lines, col), lambda i: (0, 0)),
+        in_specs=[pl.BlockSpec(memory_space=pl.ANY)] * 3,
         out_shape=jax.ShapeDtypeStruct((lines, col), BF),
         scratch_shapes=[
+            pltpu.VMEM((lines, col), BF),
+            pltpu.VMEM((2, width, hidden), BF),
+            pltpu.VMEM((hidden, width), BF),
             pltpu.VMEM((lines // Y, width), BF),
-            pltpu.VMEM((lines // Y, width), F32),
+            pltpu.SemaphoreType.DMA((4,)),
         ],
         name="run_expert",
     )(inbound, gate_up, down)
@@ -194,17 +232,9 @@
     attended = attend(mine_q, mine_kv, kv_cache, cache_len, head_dim)
     partial_value = jnp.dot(attended, attn_out_w, preferred_element_type=F32).astype(BF)
     parts = share(jnp.concatenate([partial_value, mine_res], axis=1), "y", Y)
-    full_res = jnp.concatenate([parts[t, :, width:] for t in range(Y)], axis=1).astype(F32)
-    mixed_full = full_res + jnp.sum(parts[:, :, :width].astype(F32), axis=0)
-    scale_rows = lax.rsqrt(jnp.mean(mixed_full * mixed_full, axis=1, keepdims=True) + epsilon)
-    normed = (mixed_full * scale_rows * post_gain).astype(BF)
-
     spread, blend_two = route_tables(expert_ids, route_wt, groups, cap)
     lines = groups * cap * Y
-    tall = jnp.concatenate([normed[:, t * col : (t + 1) * col] for t in range(Y)], axis=0)
-    sent = lax.dot_general(
-        spread.astype(BF), tall, (((0,), (0,)), ((), ())), preferred_element_type=F32
-    ).astype(BF)
+    mixed_full, sent = mix_rows(parts, post_gain, spread)
     inbound = lax.all_to_all(sent.reshape(groups, cap * Y, col), REQ, 0, 0, tiled=True)
     produced = run_expert(inbound.reshape(lines, col), expert_gate_up, expert_down)
 
@@ -228,6 +258,7 @@
     local_top = jnp.maximum(jnp.max(logits, axis=1), jnp.max(logits_other, axis=1))
     pick = request_perm[:, None] == slot_of[None, :]
     top_by_request = jnp.max(jnp.where(pick, local_top[None, :], -jnp.inf), axis=1)
+    swap = [(0, 1), (1, 0)]
     every, top_by_request = lax.optimization_barrier((every, top_by_request))
     tops = jnp.broadcast_to(top_by_request.reshape(groups, 1, rows), (groups, Y, rows))
     tops = lax.all_to_all(tops.reshape(groups * Y, rows), ALL, 0, 0, tiled=True)
@@ -237,7 +268,7 @@
     back = wanted[:, None] == slot_of[None, :]
     found = jnp.dot(back.astype(BF), every, preferred_element_type=F32).astype(BF)
     crossed = lax.ppermute(
-        jnp.where(ic == 0, found[rows:], found[:rows]), "c", [(0, 1), (1, 0)]
+        jnp.where(ic == 0, found[rows:], found[:rows]), "c", swap
     )
     hidden = jnp.where(ic == 0, found[:rows], found[rows:]).astype(F32) + crossed.astype(F32)
     hidden_out = lax.dynamic_slice_in_dim(hidden, iy * col, col, 1).astype(BF)

time: 191 us -> 189 us (0.990)
    pallas_call x1 -> x2, Pallas kernels: 6.81 us -> 7.25 us  [the longest x1 5.02 us: run_expert(): pl.pallas_call(expert_kernel, in_specs=[pl.BlockSpec(memory_space=pl.ANY)...]
where the time goes in v4:
time: 189 us; the launch traced here: 188 us
  blocking collectives  71.2 us (38%)
  waiting for transfers between devices  48.5 us (26%)
  starting transfers between devices  35.4 us (19%)
  matrix products  12.2 us (6%)
  Pallas kernels  8.8 us (5%)
  local copies, waits for them, and re-layouts  7.07 us (4%)
  other arithmetic  3.97 us (2%)
    all_to_all x1, blocking collectives, on_device(): lax.all_to_all(sent.reshape(groups, cap * Y, col), REQ, 0, 0, tiled=True)  29.3 us
    all_to_all x4, waiting for transfers between devices, share(): return lax.all_to_all(stacked, axes, 0, 0, tiled=True)  27.9 us
    all_to_all x1, blocking collectives, on_device(): lax.all_to_all(produced.reshape(groups, cap * Y, col), REQ, 0, 0, tiled=T...  26.6 us
    all_to_all x4, starting transfers between devices, share(): return lax.all_to_all(stacked, axes, 0, 0, tiled=True)  19 us
    all_to_all x1, blocking collectives, share(): return lax.all_to_all(stacked, axes, 0, 0, tiled=True)  15.3 us
    all_to_all x1, waiting for transfers between devices, on_device(): tops = lax.all_to_all(tops.reshape(groups * Y, rows), ALL, 0, 0, tiled=True)  12.8 us
    all_to_all x1, waiting for transfers between devices, on_device(): lax.all_to_all(outgoing.reshape(Z, rows, -1), 'z', 0, 0, tiled=True)  7.78 us
    all_to_all x1, starting transfers between devices, on_device(): lax.all_to_all(outgoing.reshape(Z, rows, -1), 'z', 0, 0, tiled=True)  7.43 us
  transfers between devices with their start and end apart: 8, of which 6 were waited for; matrix products, arithmetic and copies ran while one was open for 4% of the time, Pallas kernels for 1%

profile of v4, /device:TPU:1, one launch (start us, length us, event | category | flops | bytes accessed | tf_op | source)
XLA Modules:
  0.0 187.9 jit_solution(15454734178302253632)
XLA Ops:
  2.2 6.5 %all-to-all-start = ((bf16[8,8,1536]{2,1,0:T(8,128)(2,1)}), bf16[8,8,1536]{2,1,0:T(8,128)(2,1)S(1)}, u32[]{:S(2)}, u32[]{:S(2)}) async-start(bf16[8,8,1536]{2,1,0:T(8,128)(2,1)} %broadcast_in_dim.41), calls=%async_computation | async-start | bytes 393216 | tf_op jit(solution)/shard_map/all_to_all | solution.py:49
  9.8 4.9 %all-to-all-done = bf16[8,8,1536]{2,1,0:T(8,128)(2,1)S(1)} async-done(((bf16[8,8,1536]{2,1,0:T(8,128)(2,1)}), bf16[8,8,1536]{2,1,0:T(8,128)(2,1)S(1)}, u32[]{:S(2)}, u32[]{:S(2)}) %all-to-all-start) | async-done | bytes 196640 | tf_op jit(solution)/shard_map/all_to_all | solution.py:49
  15.6 7.4 %all-to-all-start.1 = ((bf16[8,8,1536]{2,1,0:T(8,128)(2,1)}), bf16[8,8,1536]{2,1,0:T(8,128)(2,1)S(1)}, u32[]{:S(2)}, u32[]{:S(2)}) async-start(bf16[8,8,1536]{2,1,0:T(8,128)(2,1)} %fusion), calls=%async_computation.1 | async-start | bytes 393216 | tf_op jit(solution)/shard_map/all_to_all | solution.py:226
  23.8 7.8 %all-to-all-done.1 = bf16[8,8,1536]{2,1,0:T(8,128)(2,1)S(1)} async-done(((bf16[8,8,1536]{2,1,0:T(8,128)(2,1)}), bf16[8,8,1536]{2,1,0:T(8,128)(2,1)S(1)}, u32[]{:S(2)}, u32[]{:S(2)}) %all-to-all-start.1) | async-done | bytes 196640 | tf_op jit(solution)/shard_map/all_to_all | solution.py:226
  31.7 1.7 fusion.34
  33.6 1.5 fusion.4
  36.4 4.2 %all-to-all-start.2 = ((bf16[4,8,3200]{2,1,0:T(8,128)(2,1)}), bf16[4,8,3200]{2,1,0:T(8,128)(2,1)S(1)}, u32[]{:S(2)}, u32[]{:S(2)}) async-start(bf16[4,8,3200]{2,1,0:T(8,128)(2,1)} %broadcast_in_dim.44), calls=%async_computation.2 | async-start | bytes 409600 | tf_op jit(solution)/shard_map/all_to_all | solution.py:49
  41.2 1.6 route_tables.1
  42.8 3.1 %all-to-all-done.2.parts_ref = bf16[4,8,3200]{2,1,0:T(8,128)(2,1)S(1)} async-done(((bf16[4,8,3200]{2,1,0:T(8,128)(2,1)}), bf16[4,8,3200]{2,1,0:T(8,128)(2,1)S(1)}, u32[]{:S(2)}, u32[]{:S(2)}) %all-to-all-start.2) | async-done | bytes 204832 | tf_op jit(solution)/shard_map/all_to_all | solution.py:49
  46.5 2.2 %mix_rows.1 = (f32[8,2560]{1,0:T(8,128)}, bf16[512,640]{1,0:T(8,128)(2,1)}) custom-call(bf16[4,8,3200]{2,1,0:T(8,128)(2,1)} %copy-done.1, f32[1,2560]{1,0:T(1,128)} %reshape.220.gain_ref, f32[32,512]{1,0:T(8,128)} %get-tuple-element.9.spread_ref), custom_call_target="tpu_custom_call" | custom-call | tf_op jit(solution)/shard_map/mix_rows/pallas_call | solution.py:125
  48.7 29.3 %all_to_all.49 = bf16[64,8,640]{2,1,0:T(8,128)(2,1)} all-to-all(bf16[64,8,640]{2,1,0:T(8,128)(2,1)} %bitcast.49), channel_id=1, replica_groups=mesh['x'=4,'z'=8,'c'=2,'y'=4] {'x','z','c'}, dimensions={0} | all-to-all | bytes 1310720 | tf_op jit(solution)/shard_map/all_to_all | solution.py:238
  78.1 5.0 %run_expert.1 = bf16[512,640]{1,0:T(8,128)(2,1)} custom-call(bf16[512,640]{1,0:T(8,128)(2,1)} %bitcast.47, bf16[1,2,2560,384]{3,2,1,0:T(8,128)(2,1)} %up_hbm.1, bf16[1,384,2560]{2,1,0:T(8,128)(2,1)} %down_hbm.1), custom_call_target="tpu_custom_call" | custom-call | tf_op jit(solution)/shard_map/run_expert/pallas_call | solution.py:176
  83.1 26.6 %all_to_all.50 = bf16[64,8,640]{2,1,0:T(8,128)(2,1)S(1)} all-to-all(bf16[64,8,640]{2,1,0:T(8,128)(2,1)} %bitcast.48), channel_id=1, replica_groups=mesh['x'=4,'z'=8,'c'=2,'y'=4] {'x','z','c'}, dimensions={0} | all-to-all | bytes 1310720 | tf_op jit(solution)/shard_map/all_to_all | solution.py:241
  110.7 3.3 %all-to-all-start.5 = ((bf16[4,8,2560]{2,1,0:T(8,128)(2,1)}), bf16[4,8,2560]{2,1,0:T(8,128)(2,1)S(1)}, u32[]{:S(2)}, u32[]{:S(2)}) async-start(bf16[4,8,2560]{2,1,0:T(8,128)(2,1)} %broadcast_in_dim.45), calls=%async_computation.5 | async-start | bytes 327680 | tf_op jit(solution)/shard_map/all_to_all | solution.py:49
  114.4 4.8 %all-to-all-done.5 = bf16[4,8,2560]{2,1,0:T(8,128)(2,1)S(1)} async-done(((bf16[4,8,2560]{2,1,0:T(8,128)(2,1)}), bf16[4,8,2560]{2,1,0:T(8,128)(2,1)S(1)}, u32[]{:S(2)}, u32[]{:S(2)}) %all-to-all-start.5) | async-done | bytes 163872 | tf_op jit(solution)/shard_map/all_to_all | solution.py:49
  119.3 15.3 %all_to_all.51 = bf16[8,8,2560]{2,1,0:T(8,128)(2,1)S(1)} all-to-all(bf16[8,8,2560]{2,1,0:T(8,128)(2,1)S(1)} %broadcast_in_dim.46), channel_id=1, replica_groups=mesh['x'=4,'z'=8,'c'=2,'y'=4] {'z'}, dimensions={0} | all-to-all | bytes 655360 | tf_op jit(solution)/shard_map/all_to_all | solution.py:49
  135.7 4.9 %all-to-all-start.7 = ((bf16[4,8,8,2560]{3,2,1,0:T(8,128)(2,1)}), bf16[4,8,8,2560]{3,2,1,0:T(8,128)(2,1)}, u32[]{:S(2)}, u32[]{:S(2)}) async-start(bf16[4,8,8,2560]{3,2,1,0:T(8,128)(2,1)} %broadcast_in_dim.47), calls=%async_computation.7 | async-start | bytes 2621440 | tf_op jit(solution)/shard_map/all_to_all | solution.py:49
  141.0 15.2 %all-to-all-done.7 = bf16[4,8,8,2560]{3,2,1,0:T(8,128)(2,1)} async-done(((bf16[4,8,8,2560]{3,2,1,0:T(8,128)(2,1)}), bf16[4,8,8,2560]{3,2,1,0:T(8,128)(2,1)}, u32[]{:S(2)}, u32[]{:S(2)}) %all-to-all-start.7) | async-done | bytes 1310752 | tf_op jit(solution)/shard_map/all_to_all | solution.py:49
  156.2 2.8 %convolution_reduce_fusion.1 = f32[256]{0:T(256)S(1)} fusion(bf16[404,2560]{1,0:T(8,128)(2,1)} %param.27, bf16[256,2560]{1,0:T(8,128)(2,1)} %bitcast.18, f32[2560]{0:T(1024)S(1)} %copy-done.6), kind=kOutput, calls=%fused_computation.6 | convolution fusion | flops 531600128 | bytes 3390464 | tf_op jit(solution)/shard_map/dot_general | solution.py:256
  159.0 2.8 %convolution_reduce_fusion = f32[256]{0:T(256)S(1)} fusion(bf16[404,2560]{1,0:T(8,128)(2,1)} %collective-permute-done, bf16[256,2560]{1,0:T(8,128)(2,1)} %bitcast.18, f32[2560]{0:T(1024)S(1)} %copy-done.6), kind=kOutput, calls=%fused_computation.5 | convolution fusion | flops 531600128 | bytes 3390464 | tf_op jit(solution)/shard_map/dot_general | solution.py:257
  162.0 1.6 convolution_convert_fusion
  164.2 3.4 %collective-permute-start.1 = (bf16[8,2560]{1,0:T(8,128)(2,1)}, bf16[8,2560]{1,0:T(8,128)(2,1)S(1)}, u32[]{:S(2)}, u32[]{:S(2)}) collective-permute-start(bf16[8,2560]{1,0:T(8,128)(2,1)} %broadcast_select_fusion), channel_id=1, source_target_pairs={{0,4},{4,0},{1,5},{5,1},{2,6},{6,2},{3,7},{7,3},{8,12},{12,8},{9,1... | collective-permute-start | bytes 122888 | tf_op jit(solution)/shard_map/ppermute | solution.py:270
  168.4 5.1 %all-to-all-start.8 = ((f32[256,1,8]{2,1,0:T(1,128)}), f32[256,1,8]{2,1,0:T(1,128)S(1)}, u32[]{:S(2)}, u32[]{:S(2)}) async-start(f32[256,1,8]{2,1,0:T(1,128)} %bitcast.19), calls=%async_computation.8 | async-start | bytes 262144 | tf_op jit(solution)/shard_map/all_to_all | solution.py:264
  173.6 12.8 %all-to-all-done.8 = f32[256,1,8]{2,1,0:T(1,128)S(1)} async-done(((f32[256,1,8]{2,1,0:T(1,128)}), f32[256,1,8]{2,1,0:T(1,128)S(1)}, u32[]{:S(2)}, u32[]{:S(2)}) %all-to-all-start.8) | async-done | bytes 8224 | tf_op jit(solution)/shard_map/all_to_all | solution.py:264
  (62 shorter events, 13.2 us)
Async XLA Ops:
  0.6 34.5 %copy-start = (bf16[640,2560]{1,0:T(8,128)(2,1)S(1)}, bf16[640,2560]{1,0:T(8,128)(2,1)}, u32[]{:S(2)}) copy-start(bf16[640,2560]{1,0:T(8,128)(2,1)} %param.22) | copy-start | bytes 9830404
  2.2 12.4 %all-to-all-start = ((bf16[8,8,1536]{2,1,0:T(8,128)(2,1)}), bf16[8,8,1536]{2,1,0:T(8,128)(2,1)S(1)}, u32[]{:S(2)}, u32[]{:S(2)}) async-start(bf16[8,8,1536]{2,1,0:T(8,128)(2,1)} %broadcast_in_dim.41), calls=%async_computation | async-start | bytes 393216 | tf_op jit(solution)/shard_map/all_to_all | solution.py:49
  15.6 15.9 %all-to-all-start.1 = ((bf16[8,8,1536]{2,1,0:T(8,128)(2,1)}), bf16[8,8,1536]{2,1,0:T(8,128)(2,1)S(1)}, u32[]{:S(2)}, u32[]{:S(2)}) async-start(bf16[8,8,1536]{2,1,0:T(8,128)(2,1)} %fusion), calls=%async_computation.1 | async-start | bytes 393216 | tf_op jit(solution)/shard_map/all_to_all | solution.py:226
  35.2 5.4 %copy-start.4 = (f32[2560]{0:T(1024)S(1)}, f32[2560]{0:T(1024)}, u32[]{:S(2)}) copy-start(f32[2560]{0:T(1024)} %param.23) | copy-start | bytes 30724
  36.4 9.4 %all-to-all-start.2 = ((bf16[4,8,3200]{2,1,0:T(8,128)(2,1)}), bf16[4,8,3200]{2,1,0:T(8,128)(2,1)S(1)}, u32[]{:S(2)}, u32[]{:S(2)}) async-start(bf16[4,8,3200]{2,1,0:T(8,128)(2,1)} %broadcast_in_dim.44), calls=%async_computation.2 | async-start | bytes 409600 | tf_op jit(solution)/shard_map/all_to_all | solution.py:49
  45.8 0.7 copy-start.1
  78.1 31.7 %copy-start.2 = (f32[64,512]{1,0:T(8,128)S(1)}, f32[64,512]{1,0:T(8,128)}, u32[]{:S(2)}) copy-start(f32[64,512]{1,0:T(8,128)} %get-tuple-element.11) | copy-start | bytes 393220
  83.1 36.1 %copy-start.3 = (f32[8,2560]{1,0:T(8,128)S(1)}, f32[8,2560]{1,0:T(8,128)}, u32[]{:S(2)}) copy-start(f32[8,2560]{1,0:T(8,128)} %get-tuple-element.10) | copy-start | bytes 245764
  110.7 8.5 %all-to-all-start.5 = ((bf16[4,8,2560]{2,1,0:T(8,128)(2,1)}), bf16[4,8,2560]{2,1,0:T(8,128)(2,1)S(1)}, u32[]{:S(2)}, u32[]{:S(2)}) async-start(bf16[4,8,2560]{2,1,0:T(8,128)(2,1)} %broadcast_in_dim.45), calls=%async_computation.5 | async-start | bytes 327680 | tf_op jit(solution)/shard_map/all_to_all | solution.py:49
  114.1 44.9 %collective-permute-start = (bf16[404,2560]{1,0:T(8,128)(2,1)}, bf16[404,2560]{1,0:T(8,128)(2,1)}, u32[]{:S(2)}, u32[]{:S(2)}) collective-permute-start(bf16[404,2560]{1,0:T(8,128)(2,1)} %param.27), channel_id=1, source_target_pairs={{0,4},{4,0},{1,5},{5,1},{2,6},{6,2},{3,7},{7,3},{8,12},{12,8},{9,1... | collective-permute-start | bytes 6205448 | tf_op jit(solution)/shard_map/ppermute | solution.py:207
  134.5 6.3 %copy-start.5 = (s32[512]{0:T(512)S(1)}, s32[512]{0:T(512)}, u32[]{:S(2)}) copy-start(s32[512]{0:T(512)} %param.19) | copy-start | bytes 6148
  134.5 21.7 %copy-start.6 = (f32[2560]{0:T(1024)S(1)}, f32[2560]{0:T(1024)}, u32[]{:S(2)}) copy-start(f32[2560]{0:T(1024)} %param.26) | copy-start | bytes 30724
  135.7 20.5 %all-to-all-start.7 = ((bf16[4,8,8,2560]{3,2,1,0:T(8,128)(2,1)}), bf16[4,8,8,2560]{3,2,1,0:T(8,128)(2,1)}, u32[]{:S(2)}, u32[]{:S(2)}) async-start(bf16[4,8,8,2560]{3,2,1,0:T(8,128)(2,1)} %broadcast_in_dim.47), calls=%async_computation.7 | async-start | bytes 2621440 | tf_op jit(solution)/shard_map/all_to_all | solution.py:49
  164.2 22.4 %collective-permute-start.1 = (bf16[8,2560]{1,0:T(8,128)(2,1)}, bf16[8,2560]{1,0:T(8,128)(2,1)S(1)}, u32[]{:S(2)}, u32[]{:S(2)}) collective-permute-start(bf16[8,2560]{1,0:T(8,128)(2,1)} %broadcast_select_fusion), channel_id=1, source_target_pairs={{0,4},{4,0},{1,5},{5,1},{2,6},{6,2},{3,7},{7,3},{8,12},{12,8},{9,1... | collective-permute-start | bytes 122888 | tf_op jit(solution)/shard_map/ppermute | solution.py:270
  168.4 17.9 %all-to-all-start.8 = ((f32[256,1,8]{2,1,0:T(1,128)}), f32[256,1,8]{2,1,0:T(1,128)S(1)}, u32[]{:S(2)}, u32[]{:S(2)}) async-start(f32[256,1,8]{2,1,0:T(1,128)} %bitcast.19), calls=%async_computation.8 | async-start | bytes 262144 | tf_op jit(solution)/shard_map/all_to_all | solution.py:264
